TPU v7x, 32 devices: a whole 2x2x4 slice. The times are simulated.
32 devices in a mesh: chan: 8 (over y, x, core), slab: 4 (over z).
Axes of the slice: x: 2, y: 2, z: 4, core: 2. Of those that a mesh axis runs over, the one named last changes fastest.
Arguments:
- activations: bfloat16 [128, 8, 8, 128], P('chan', 'slab'), may hold values from -6 to 6
- cotangent: bfloat16 [128, 8, 8, 128], P('chan', 'slab'), may hold values from -6 to 6
- relu_mask: int32 [128, 8, 8, 128], P('chan', 'slab'), may hold values 0 or 1
- weights: bfloat16 [3, 3, 3, 128, 128], replicated, may hold values from -0.109375 to 0.109375
Outputs:
- pre: bfloat16 [128, 8, 8, 128], P('chan', 'slab')
- grad_input: bfloat16 [128, 8, 8, 128], P('chan', 'slab')
All inputs are finite; a program needn't handle non-finite values. No bound on the sum of `relu_mask` on one device may be relied on, other than what follows from the above.
Results may differ from a plain program's by a relative error of at most 0.0013.
Values may be sent and summed in bfloat16 or wider, within the bound.
No kernel may reach another device: no remote copies, remote signals or barrier semaphores. Data moves between devices by JAX's collectives and lax.ppermute only.
A program may use at most 64 MiB of HBM per device.

v0:
```python
import jax
import jax.numpy as jnp
from jax import lax
from jax.sharding import PartitionSpec as P


def with_halo(shard, sides, width):
    for axis, dim in sides:
        devices, length = (lax.axis_size(axis), shard.shape[dim])
        up = [(i, (i + 1) % devices) for i in range(devices - 1)]
        down = [(j, i) for i, j in up]
        last = lax.slice_in_dim(shard, length - width, length, axis=dim)
        first = lax.slice_in_dim(shard, 0, width, axis=dim)
        before = lax.ppermute(last, axis, up)
        after = lax.ppermute(first, axis, down)
        shard = jnp.concatenate([before, shard, after], axis=dim)
    return shard


def offset_list():
    return [(i, j, k) for i in range(3) for j in range(3) for k in range(3)]


def tap_windows(padded, planes, height, breadth, flipped):
    pieces = []
    for i, j, k in offset_list():
        if flipped:
            pieces.append(
                padded[:, 2 - i : 2 - i + planes, 2 - j : 2 - j + height, 2 - k : 2 - k + breadth]
            )
        else:
            pieces.append(padded[:, i : i + planes, j : j + height, k : k + breadth])
    return pieces


def forward_sum(w_rows, padded, planes, height, breadth):
    windows = tap_windows(padded, planes, height, breadth, False)
    total = jnp.zeros((w_rows.shape[3], planes, height, breadth), jnp.float32)
    for tap, (i, j, k) in enumerate(offset_list()):
        total = total + jnp.einsum(
            "oi,idhw->odhw", w_rows[i, j, k], windows[tap], preferred_element_type=jnp.float32
        )
    return total


def backward_sum(w_cols, padded, planes, height, breadth):
    outputs = w_cols.shape[4]
    windows = tap_windows(padded, planes, height, breadth, True)
    total = jnp.zeros((outputs, planes, height, breadth), jnp.float32)
    for tap, (i, j, k) in enumerate(offset_list()):
        total = total + jnp.einsum(
            "oi,odhw->idhw", w_cols[i, j, k], windows[tap], preferred_element_type=jnp.float32
        )
    return total


def body(activations, cotangent, relu_mask, weights):
    planes = activations.shape[1]
    breadth = activations.shape[3]
    masked = jnp.where(relu_mask == 1, cotangent, jnp.zeros_like(cotangent))
    stacked = jnp.stack([activations, masked])
    patches = lax.all_to_all(stacked, "chan", split_axis=3, concat_axis=1, tiled=True)
    rimmed = with_halo(patches, (("chan", 3), ("slab", 2)), 1)
    padded = jnp.pad(rimmed, ((0, 0), (0, 0), (0, 0), (0, 0), (1, 1)))
    row_block = patches.shape[3]
    pre_block = forward_sum(weights, padded[0], planes, row_block, breadth).astype(jnp.bfloat16)
    grad_block = backward_sum(weights, padded[1], planes, row_block, breadth).astype(jnp.bfloat16)
    pre, grad_input = (
        lax.all_to_all(pre_block, "chan", split_axis=0, concat_axis=2, tiled=True),
        lax.all_to_all(grad_block, "chan", split_axis=0, concat_axis=2, tiled=True),
    )
    return (pre, grad_input)


def solution(mesh):
    placed = (
        P("chan", "slab", None, None),
        P("chan", "slab", None, None),
        P("chan", "slab", None, None),
        P(),
    )
    return jax.shard_map(
        body,
        mesh=mesh,
        in_specs=placed,
        out_specs=(P("chan", "slab", None, None), P("chan", "slab", None, None)),
        check_vma=False,
    )
```

profile of v0, /device:TPU:0, one launch (start us, length us, event | category | flops | bytes accessed | tf_op | source)
XLA Modules:
  0.0 57.3 jit_solution(1241521962883106001)
XLA Ops:
  0.6 1.0 %fusion.33 = (bf16[1,16,2,8,128]{4,1,2,0,3:T(8,128)(2,1)S(1)}, bf16[1,16,2,8,128]{4,1,2,0,3:T(8,128)(2,1)S(1)}) fusion(s32[16,2,8,128]{3,2,1,0:T(8,128)} %param.6, bf16[16,2,8,128]{3,2,1,0:T(8,128)(2,1)} %param.5, bf16[16,2,8,128]{3,2,1,0:T(8,128)(2,1)} %param.4), kind=kLoop, calls=%fused_computation.94 | loop fusion | flops 65536 | bytes 393216 | tf_op jit(solution)/shard_map/stack | solution.py:61
  1.7 10.5 %all_to_all.54 = bf16[2,16,2,8,128]{4,1,2,0,3:T(8,128)(2,1)S(1)} all-to-all(bf16[2,16,2,8,128]{4,1,2,0,3:T(8,128)(2,1)S(1)} %pad_maximum_fusion.1), channel_id=1, replica_groups=mesh['chan'=8,'slab'=4] {'chan'}, dimensions={3} | all-to-all | bytes 262144 | tf_op jit(solution)/shard_map/all_to_all | solution.py:62
  12.3 1.3 %collective-permute-start.1 = (bf16[2,128,2,1,128]{1,4,2,3,0:T(8,128)(2,1)S(1)}, bf16[2,128,2,1,128]{1,4,2,3,0:T(8,128)(2,1)S(1)}, u32[]{:S(2)}, u32[]{:S(2)}) collective-permute-start(bf16[2,128,2,1,128]{1,4,2,3,0:T(8,128)(2,1)S(1)} %copy.23), channel_id=1, source_target_pairs={{4,0},{8,4},{12,8},{16,12},{20,16},{24,20},{28,24},{5,1},{9,5},{13... | collective-permute-start | bytes 393224 | tf_op jit(solution)/shard_map/ppermute | solution.py:15
  13.6 3.0 %collective-permute-start = (bf16[2,128,2,1,128]{1,4,2,3,0:T(8,128)(2,1)S(1)}, bf16[2,128,2,1,128]{1,4,2,3,0:T(8,128)(2,1)S(1)}, u32[]{:S(2)}, u32[]{:S(2)}) collective-permute-start(bf16[2,128,2,1,128]{1,4,2,3,0:T(8,128)(2,1)S(1)} %copy.23), channel_id=1, source_target_pairs={{0,4},{4,8},{8,12},{12,16},{16,20},{20,24},{24,28},{1,5},{5,9},{9,... | collective-permute-start | bytes 393224 | tf_op jit(solution)/shard_map/ppermute | solution.py:14
  16.7 1.0 %collective-permute-done = bf16[2,128,2,1,128]{1,4,2,3,0:T(8,128)(2,1)S(1)} collective-permute-done((bf16[2,128,2,1,128]{1,4,2,3,0:T(8,128)(2,1)S(1)}, bf16[2,128,2,1,128]{1,4,2,3,0:T(8,128)(2,1)S(1)}, u32[]{:S(2)}, u32[]{:S(2)}) %collective-permute-start) | collective-permute-done | bytes 131104 | tf_op jit(solution)/shard_map/ppermute | solution.py:14
  17.7 3.5 %collective-permute-start.2 = (bf16[2,128,1,3,128]{1,4,2,3,0:T(8,128)(2,1)S(1)}, bf16[2,128,1,3,128]{1,4,2,3,0:T(8,128)(2,1)S(1)}, u32[]{:S(2)}, u32[]{:S(2)}) collective-permute-start(bf16[2,128,1,3,128]{1,4,2,3,0:T(8,128)(2,1)S(1)} %get-tuple-element.8), channel_id=1, source_target_pairs={{0,1},{1,2},{2,3},{4,5},{5,6},{6,7},{8,9},{9,10},{10,11},{12,13},{... | collective-permute-start | bytes 589832 | tf_op jit(solution)/shard_map/ppermute | solution.py:14
  21.2 1.3 %collective-permute-start.3 = (bf16[2,128,1,3,128]{1,4,2,3,0:T(8,128)(2,1)S(1)}, bf16[2,128,1,3,128]{1,4,2,3,0:T(8,128)(2,1)S(1)}, u32[]{:S(2)}, u32[]{:S(2)}) collective-permute-start(bf16[2,128,1,3,128]{1,4,2,3,0:T(8,128)(2,1)S(1)} %get-tuple-element.9), channel_id=1, source_target_pairs={{1,0},{2,1},{3,2},{5,4},{6,5},{7,6},{9,8},{10,9},{11,10},{13,12},{... | collective-permute-start | bytes 589832 | tf_op jit(solution)/shard_map/ppermute | solution.py:15
  22.5 3.2 %collective-permute-done.2 = bf16[2,128,1,3,128]{1,4,2,3,0:T(8,128)(2,1)S(1)} collective-permute-done((bf16[2,128,1,3,128]{1,4,2,3,0:T(8,128)(2,1)S(1)}, bf16[2,128,1,3,128]{1,4,2,3,0:T(8,128)(2,1)S(1)}, u32[]{:S(2)}, u32[]{:S(2)}) %collective-permute-start.2) | collective-permute-done | bytes 196640 | tf_op jit(solution)/shard_map/ppermute | solution.py:14
  25.7 4.7 %collective-permute-done.3 = bf16[2,128,1,3,128]{1,4,2,3,0:T(8,128)(2,1)S(1)} collective-permute-done((bf16[2,128,1,3,128]{1,4,2,3,0:T(8,128)(2,1)S(1)}, bf16[2,128,1,3,128]{1,4,2,3,0:T(8,128)(2,1)S(1)}, u32[]{:S(2)}, u32[]{:S(2)}) %collective-permute-start.3) | collective-permute-done | bytes 196640 | tf_op jit(solution)/shard_map/ppermute | solution.py:15
  30.4 0.3 select_maximum_fusion
  30.7 1.1 %copy-done = bf16[3,3,3,128,128]{4,3,2,1,0:T(8,128)(2,1)S(1)} copy-done((bf16[3,3,3,128,128]{4,3,2,1,0:T(8,128)(2,1)S(1)}, bf16[3,3,3,128,128]{4,3,2,1,0:T(8,128)(2,1)}, u32[]{:S(2)}) %copy-start) | copy-done | bytes 884760
  32.0 0.1 convolution_bitcast_fusion.1
  32.9 0.1 convolution_bitcast_fusion.7
  33.3 0.2 convolution_bitcast_fusion.10
  33.5 0.2 convolution_bitcast_fusion.11
  33.7 0.2 convolution_bitcast_fusion.12
  33.9 0.2 convolution_bitcast_fusion.13
  34.0 0.2 convolution_bitcast_fusion.14
  34.2 0.2 convolution_bitcast_fusion.15
  34.4 0.2 convolution_bitcast_fusion.16
  34.5 0.2 convolution_bitcast_fusion.17
  34.7 0.2 convolution_bitcast_fusion.18
  34.9 0.2 fusion.35
  35.0 0.2 convolution_add_fusion.15
  35.2 0.1 convolution_add_fusion.14
  35.3 0.1 convolution_add_fusion.13
  35.5 0.2 convolution_add_fusion.12
  35.6 0.2 convolution_add_fusion.11
  35.8 0.1 convolution_add_fusion.10
  36.0 0.2 convolution_add_fusion.9
  36.1 0.2 convolution_add_fusion.8
  36.3 0.1 convolution_add_fusion.7
  36.4 0.2 convolution_add_fusion.6
  36.6 0.2 convolution_add_fusion.5
  36.7 0.1 convolution_add_fusion.4
  36.9 0.1 convolution_add_fusion.3
  37.2 0.2 convolution_add_fusion.1
  37.3 0.2 fusion.21
  37.5 0.2 fusion.26
  37.7 0.8 %copy.28 = bf16[128,2,1,128]{3,1,2,0:T(2,128)(2,1)} copy(bf16[128,2,1,128]{0,3,1,2:T(8,128)(2,1)S(1)} %fusion.26) | data formatting | bytes 131072 | tf_op jit(solution)/shard_map/convert_element_type | solution.py:67
  38.5 4.8 %all-to-all-start.2 = ((bf16[128,2,1,128]{3,1,2,0:T(2,128)(2,1)}), bf16[128,2,1,128]{3,1,2,0:T(2,128)(2,1)S(1)}, u32[]{:S(2)}, u32[]{:S(2)}) async-start(bf16[128,2,1,128]{3,1,2,0:T(2,128)(2,1)} %copy.28), calls=%async_computation.2 | async-start | bytes 131072 | tf_op jit(solution)/shard_map/all_to_all | solution.py:70
  43.3 0.2 convolution_add_fusion.31
  43.5 0.2 convolution_add_fusion.30
  43.6 0.2 convolution_add_fusion.29
  43.8 0.2 convolution_add_fusion.28
  44.0 0.2 convolution_add_fusion.27
  44.1 0.2 convolution_add_fusion.26
  44.3 0.2 convolution_add_fusion.25
  44.5 0.2 convolution_add_fusion.24
  44.7 0.2 convolution_add_fusion.23
  44.8 0.2 convolution_add_fusion.22
  45.0 0.2 convolution_add_fusion.21
  45.2 0.2 convolution_add_fusion.20
  45.3 0.2 convolution_add_fusion.19
  45.5 0.2 convolution_add_fusion.18
  45.7 0.2 convolution_add_fusion.17
  45.9 0.2 fusion.22
  46.0 0.2 fusion.25
  46.3 0.8 %copy.26 = bf16[128,2,1,128]{3,1,2,0:T(2,128)(2,1)} copy(bf16[128,2,1,128]{0,3,1,2:T(8,128)(2,1)S(1)} %fusion.25) | data formatting | bytes 131072 | tf_op jit(solution)/shard_map/convert_element_type | solution.py:66
  47.0 1.3 %all-to-all-done.2 = bf16[128,2,1,128]{3,1,2,0:T(2,128)(2,1)S(1)} async-done(((bf16[128,2,1,128]{3,1,2,0:T(2,128)(2,1)}), bf16[128,2,1,128]{3,1,2,0:T(2,128)(2,1)S(1)}, u32[]{:S(2)}, u32[]{:S(2)}) %all-to-all-start.2) | async-done | bytes 65568 | tf_op jit(solution)/shard_map/all_to_all | solution.py:70
  48.3 3.4 %all-to-all-start.1 = ((bf16[128,2,1,128]{3,1,2,0:T(2,128)(2,1)}), bf16[128,2,1,128]{3,1,2,0:T(2,128)(2,1)S(1)}, u32[]{:S(2)}, u32[]{:S(2)}) async-start(bf16[128,2,1,128]{3,1,2,0:T(2,128)(2,1)} %copy.26), calls=%async_computation.1 | async-start | bytes 131072 | tf_op jit(solution)/shard_map/all_to_all | solution.py:69
  51.7 0.6 %copy.31 = bf16[16,2,8,128]{3,2,1,0:T(8,128)(2,1)} copy(bf16[16,2,8,128]{3,0,2,1:T(8,128)(2,1)S(1)} %bitcast.471) | data formatting | bytes 131072
  52.3 4.3 %all-to-all-done.1 = bf16[128,2,1,128]{3,1,2,0:T(2,128)(2,1)S(1)} async-done(((bf16[128,2,1,128]{3,1,2,0:T(2,128)(2,1)}), bf16[128,2,1,128]{3,1,2,0:T(2,128)(2,1)S(1)}, u32[]{:S(2)}, u32[]{:S(2)}) %all-to-all-start.1) | async-done | bytes 65568 | tf_op jit(solution)/shard_map/all_to_all | solution.py:69
  56.6 0.6 %copy.30 = bf16[16,2,8,128]{3,2,1,0:T(8,128)(2,1)} copy(bf16[16,2,8,128]{3,0,2,1:T(8,128)(2,1)S(1)} %bitcast.472) | data formatting | bytes 131072
  (19 shorter events, 1.6 us)
Async XLA Ops:
  12.3 4.3 %collective-permute-start.1 = (bf16[2,128,2,1,128]{1,4,2,3,0:T(8,128)(2,1)S(1)}, bf16[2,128,2,1,128]{1,4,2,3,0:T(8,128)(2,1)S(1)}, u32[]{:S(2)}, u32[]{:S(2)}) collective-permute-start(bf16[2,128,2,1,128]{1,4,2,3,0:T(8,128)(2,1)S(1)} %copy.23), channel_id=1, source_target_pairs={{4,0},{8,4},{12,8},{16,12},{20,16},{24,20},{28,24},{5,1},{9,5},{13... | collective-permute-start | bytes 393224 | tf_op jit(solution)/shard_map/ppermute | solution.py:15
  13.6 4.0 %collective-permute-start = (bf16[2,128,2,1,128]{1,4,2,3,0:T(8,128)(2,1)S(1)}, bf16[2,128,2,1,128]{1,4,2,3,0:T(8,128)(2,1)S(1)}, u32[]{:S(2)}, u32[]{:S(2)}) collective-permute-start(bf16[2,128,2,1,128]{1,4,2,3,0:T(8,128)(2,1)S(1)} %copy.23), channel_id=1, source_target_pairs={{0,4},{4,8},{8,12},{12,16},{16,20},{20,24},{24,28},{1,5},{5,9},{9,... | collective-permute-start | bytes 393224 | tf_op jit(solution)/shard_map/ppermute | solution.py:14
  17.7 8.0 %collective-permute-start.2 = (bf16[2,128,1,3,128]{1,4,2,3,0:T(8,128)(2,1)S(1)}, bf16[2,128,1,3,128]{1,4,2,3,0:T(8,128)(2,1)S(1)}, u32[]{:S(2)}, u32[]{:S(2)}) collective-permute-start(bf16[2,128,1,3,128]{1,4,2,3,0:T(8,128)(2,1)S(1)} %get-tuple-element.8), channel_id=1, source_target_pairs={{0,1},{1,2},{2,3},{4,5},{5,6},{6,7},{8,9},{9,10},{10,11},{12,13},{... | collective-permute-start | bytes 589832 | tf_op jit(solution)/shard_map/ppermute | solution.py:14
  21.2 9.2 %collective-permute-start.3 = (bf16[2,128,1,3,128]{1,4,2,3,0:T(8,128)(2,1)S(1)}, bf16[2,128,1,3,128]{1,4,2,3,0:T(8,128)(2,1)S(1)}, u32[]{:S(2)}, u32[]{:S(2)}) collective-permute-start(bf16[2,128,1,3,128]{1,4,2,3,0:T(8,128)(2,1)S(1)} %get-tuple-element.9), channel_id=1, source_target_pairs={{1,0},{2,1},{3,2},{5,4},{6,5},{7,6},{9,8},{10,9},{11,10},{13,12},{... | collective-permute-start | bytes 589832 | tf_op jit(solution)/shard_map/ppermute | solution.py:15
  30.7 1.2 %copy-start = (bf16[3,3,3,128,128]{4,3,2,1,0:T(8,128)(2,1)S(1)}, bf16[3,3,3,128,128]{4,3,2,1,0:T(8,128)(2,1)}, u32[]{:S(2)}) copy-start(bf16[3,3,3,128,128]{4,3,2,1,0:T(8,128)(2,1)} %param.7) | copy-start | bytes 2654212
  38.5 9.9 %all-to-all-start.2 = ((bf16[128,2,1,128]{3,1,2,0:T(2,128)(2,1)}), bf16[128,2,1,128]{3,1,2,0:T(2,128)(2,1)S(1)}, u32[]{:S(2)}, u32[]{:S(2)}) async-start(bf16[128,2,1,128]{3,1,2,0:T(2,128)(2,1)} %copy.28), calls=%async_computation.2 | async-start | bytes 131072 | tf_op jit(solution)/shard_map/all_to_all | solution.py:70
  48.3 8.3 %all-to-all-start.1 = ((bf16[128,2,1,128]{3,1,2,0:T(2,128)(2,1)}), bf16[128,2,1,128]{3,1,2,0:T(2,128)(2,1)S(1)}, u32[]{:S(2)}, u32[]{:S(2)}) async-start(bf16[128,2,1,128]{3,1,2,0:T(2,128)(2,1)} %copy.26), calls=%async_computation.1 | async-start | bytes 131072 | tf_op jit(solution)/shard_map/all_to_all | solution.py:69
where the time goes:
time: 57.7 us; the launch traced here: 57.3 us
  starting transfers between devices  17.3 us (30%)
  waiting for transfers between devices  14.4 us (25%)
  blocking collectives  10.5 us (18%)
  matrix products  8.48 us (15%)
  local copies, waits for them, and re-layouts  4.16 us (7%)
  other arithmetic  1.35 us (2%)
  between operations  1.08 us (2%)
    all_to_all x1, blocking collectives, body(): lax.all_to_all(stacked, 'chan', split_axis=3, concat_axis=1, tiled=True)  10.5 us
    ppermute x2, starting transfers between devices, with_halo(): before = lax.ppermute(last, axis, up)  6.53 us
    all_to_all x1, starting transfers between devices, body(): lax.all_to_all(grad_block, 'chan', split_axis=0, concat_axis=2, tiled=True)  4.84 us
    ppermute x2, waiting for transfers between devices, with_halo(): after = lax.ppermute(first, axis, down)  4.69 us
    dot_general x27, matrix products, forward_sum(): jnp.einsum('oi,idhw->odhw', w_rows[i, j, k], windows[tap], preferred_elem...  4.47 us
    all_to_all x1, waiting for transfers between devices, body(): lax.all_to_all(pre_block, 'chan', split_axis=0, concat_axis=2, tiled=True)  4.28 us
    ppermute x2, waiting for transfers between devices, with_halo(): before = lax.ppermute(last, axis, up)  4.15 us
    dot_general x27, matrix products, backward_sum(): jnp.einsum('oi,odhw->idhw', w_cols[i, j, k], windows[tap], preferred_elem...  4.02 us
  transfers between devices with their start and end apart: 6, of which 5 were waited for; matrix products, arithmetic and copies ran while one was open for 7% of the time, Pallas kernels for 0%

commit v1 on v0

v1 whole, which is shorter than its diff:
```python
import functools

import jax
import jax.numpy as jnp
from jax import lax
from jax.experimental import pallas as pl
from jax.experimental.pallas import tpu as pltpu
from jax.sharding import PartitionSpec as P

LANES = 128
TILE = 16
F32 = jnp.float32


def with_halo(shard, sides, width):
    for axis, dim in sides:
        devices, length = (lax.axis_size(axis), shard.shape[dim])
        up = [(i, (i + 1) % devices) for i in range(devices - 1)]
        down = [(j, i) for i, j in up]
        last = lax.slice_in_dim(shard, length - width, length, axis=dim)
        first = lax.slice_in_dim(shard, 0, width, axis=dim)
        before = lax.ppermute(last, axis, up)
        after = lax.ppermute(first, axis, down)
        shard = jnp.concatenate([before, shard, after], axis=dim)
    return shard


def tap_sum(weights, padded, planes, height, breadth, equation, flipped):
    total = None
    for i in range(3):
        for j in range(3):
            for k in range(3):
                a, b, c = (2 - i, 2 - j, 2 - k) if flipped else (i, j, k)
                window = padded[:, a : a + planes, b : b + height, c : c + breadth]
                term = jnp.einsum(equation, weights[i, j, k], window, preferred_element_type=F32)
                total = term if total is None else total + term
    return total.astype(jnp.bfloat16)


def general_body(activations, cotangent, relu_mask, weights):
    planes, breadth = activations.shape[1], activations.shape[3]
    masked = jnp.where(relu_mask == 1, cotangent, jnp.zeros_like(cotangent))
    stacked = jnp.stack([activations, masked])
    patches = lax.all_to_all(stacked, "chan", split_axis=3, concat_axis=1, tiled=True)
    rimmed = with_halo(patches, (("chan", 3), ("slab", 2)), 1)
    padded = jnp.pad(rimmed, ((0, 0), (0, 0), (0, 0), (0, 0), (1, 1)))
    height = patches.shape[3]
    pre = tap_sum(weights, padded[0], planes, height, breadth, "oi,idhw->odhw", False)
    grad = tap_sum(weights, padded[1], planes, height, breadth, "oi,odhw->idhw", True)
    return tuple(
        lax.all_to_all(block, "chan", split_axis=0, concat_axis=2, tiled=True) for block in (pre, grad)
    )


def conv_kernel(width, sources, *refs):
    count = len(sources)
    blocks, lhs_ref = refs[:count], refs[count]
    even_ref, odd_ref, inner_ref, x_ref = refs[count + 1 :]
    arrays, rows, planes, _, cols = inner_ref.shape
    me = lax.axis_index("chan")
    even = lax.rem(lax.axis_index("slab"), 2) == 0
    channels = x_ref.shape[2]

    zero = jnp.zeros((channels, planes * cols), jnp.bfloat16)
    for a in range(arrays):
        x_ref[a, 0] = zero
        x_ref[a, rows + 1] = zero
    for block, source in zip(blocks, sources):
        where = pl.ds(pl.multiple_of(jnp.bitwise_xor(me, source) * width, width), width)
        for a in range(arrays):
            for r in range(rows):
                for p in range(planes):
                    x_ref[a, r + 1, where, p * cols : (p + 1) * cols] = block[a, r, p]

    lane = lax.broadcasted_iota(jnp.int32, (width, cols), 1)
    first, last = lane == 0, lane == cols - 1

    def columns(left, mid, right):
        left = jnp.where(first, 0.0, pltpu.roll(left, 1, 1))
        right = jnp.where(last, 0.0, pltpu.roll(right, cols - 1, 1))
        return left + mid + right

    for a in range(arrays):
        lhs = lhs_ref[a]
        for r in range(rows):
            window = x_ref[a, r : r + 3].reshape(3 * channels, planes * cols)
            y = jnp.dot(lhs, window, preferred_element_type=F32)

            def part(t, k, p):
                top = (t * 3 + k) * width
                return y[top : top + width, p * cols : (p + 1) * cols]

            outs = {}
            for q in range(-1, planes + 1):
                taps = [
                    functools.reduce(
                        lambda u, v: u + v,
                        [part(p - q + 1, k, p) for p in range(planes) if 0 <= p - q + 1 <= 2],
                    )
                    for k in range(3)
                ]
                outs[q] = columns(*taps)
            even_ref[a, r] = jnp.where(even, outs[planes], outs[-1])
            odd_ref[a, r] = jnp.where(even, outs[-1], outs[planes])
            for p in range(planes):
                inner_ref[a, r, p] = outs[p]


def add_kernel(inner_ref, even_ref, odd_ref, pre_ref, grad_ref, turned_ref):
    arrays, rows, planes, width, cols = inner_ref.shape
    even = lax.rem(lax.axis_index("slab"), 2) == 0
    for a, out_ref in enumerate((pre_ref, grad_ref)):
        for p in range(planes):
            for r in range(rows):
                value = inner_ref[a, r, p]
                if p == 0:
                    value = value + jnp.where(even, odd_ref[a, r], even_ref[a, r])
                if p == planes - 1:
                    value = value + jnp.where(even, even_ref[a, r], odd_ref[a, r])
                turned_ref[pl.ds(r, width, stride=rows), :] = value
            out_ref[:, p] = turned_ref[...].reshape(width, rows, cols).astype(jnp.bfloat16)


def aligned_body(activations, cotangent, relu_mask, weights):
    width, planes, rows, cols = activations.shape
    devices, slabs = lax.axis_size("chan"), lax.axis_size("slab")
    channels = width * devices
    masked = jnp.where(relu_mask == 1, cotangent, jnp.zeros_like(cotangent))
    own = jnp.stack([activations, masked]).transpose(0, 3, 2, 1, 4)

    def swap(value, bit):
        return lax.ppermute(value, "chan", [(i, i ^ bit) for i in range(devices)])

    far = list(range(2, devices, 2))
    near = [own] + [swap(own, bit) for bit in far]
    other = swap(jnp.stack(near), 1)
    sources = [0] + far + [1] + [bit + 1 for bit in far]
    blocks = near + [other[i] for i in range(len(near))]

    start = lax.axis_index("chan") * width
    forward = lax.dynamic_slice_in_dim(weights, start, width, 3)
    backward = lax.dynamic_slice_in_dim(weights, start, width, 4)[::-1, ::-1, ::-1].swapaxes(3, 4)
    lhs = jnp.stack([forward, backward]).transpose(0, 1, 3, 4, 2, 5)
    lhs = lhs.reshape(2, 9 * width, 3 * channels)

    edge = jax.ShapeDtypeStruct((2, rows, width, cols), F32)
    even, odd, inner = pl.pallas_call(
        functools.partial(conv_kernel, width, sources),
        out_shape=(edge, edge, jax.ShapeDtypeStruct((2, rows, planes, width, cols), F32)),
        in_specs=[pl.BlockSpec(memory_space=pltpu.VMEM)] * (len(blocks) + 1),
        out_specs=[pl.BlockSpec(memory_space=pltpu.VMEM)] * 3,
        scratch_shapes=[pltpu.VMEM((2, rows + 2, channels, planes * cols), jnp.bfloat16)],
        name="conv",
    )(*blocks, lhs)

    evens = [(i, i + 1) for i in range(0, slabs - 1, 2)]
    odds = [(i, i + 1) for i in range(1, slabs - 1, 2)]
    even, odd = (
        lax.ppermute(v, "slab", pairs + [(j, i) for i, j in pairs]) for v, pairs in ((even, evens), (odd, odds))
    )
    out = jax.ShapeDtypeStruct(activations.shape, jnp.bfloat16)
    return tuple(
        pl.pallas_call(
            add_kernel,
            out_shape=(out, out),
            in_specs=[pl.BlockSpec(memory_space=pltpu.VMEM)] * 3,
            out_specs=[pl.BlockSpec(memory_space=pltpu.VMEM)] * 2,
            scratch_shapes=[pltpu.VMEM((width * rows, cols), F32)],
            name="add",
        )(inner, even, odd)
    )


def body(activations, cotangent, relu_mask, weights):
    width, planes, rows, cols = activations.shape
    devices = lax.axis_size("chan")
    aligned = (
        width % TILE == 0
        and cols == LANES
        and devices & (devices - 1) == 0
        and devices > 1
        and planes >= 2
        and rows % 8 == 0
        and lax.axis_size("slab") > 1
    )
    return (aligned_body if aligned else general_body)(activations, cotangent, relu_mask, weights)


def solution(mesh):
    placed = P("chan", "slab", None, None)
    return jax.shard_map(
        body,
        mesh=mesh,
        in_specs=(placed, placed, placed, P()),
        out_specs=(placed, placed),
        check_vma=False,
    )
```

time: 57.7 us -> 29.4 us (0.51)
  the two profiles are of different devices: /device:TPU:0 before, /device:TPU:16 now
where the time goes in v1:
time: 29.4 us; the launch traced here: 29.2 us
  waiting for transfers between devices  11.6 us (39%)
  starting transfers between devices  7.04 us (24%)
  Pallas kernels  4.94 us (17%)
  local copies, waits for them, and re-layouts  3.73 us (13%)
  other arithmetic  1.21 us (4%)
  between operations  0.74 us (3%)
    ppermute x4, waiting for transfers between devices, swap(): return lax.ppermute(value, 'chan', [(i, i ^ bit) for i in range(devices)])  5.98 us
    ppermute x2, waiting for transfers between devices, aligned_body(): lax.ppermute(v, 'slab', pairs + [(j, i) for i, j in pairs])  5.6 us
    ppermute x4, starting transfers between devices, swap(): return lax.ppermute(value, 'chan', [(i, i ^ bit) for i in range(devices)])  3.56 us
    ppermute x2, starting transfers between devices, aligned_body(): lax.ppermute(v, 'slab', pairs + [(j, i) for i, j in pairs])  3.49 us
    pallas_call x1, Pallas kernels, aligned_body(): pl.pallas_call(functools.partial(conv_kernel, width, sources), out_shape=...  3.18 us
    pallas_call x1, Pallas kernels, aligned_body(): pl.pallas_call(add_kernel, out_shape=(out, out), in_specs=[pl.BlockSpec(m...  1.76 us
    unnamed x15, local copies, waits for them, and re-layouts  1.57 us
    another operation x1, other arithmetic, aligned_body(): own = jnp.stack([activations, masked]).transpose(0, 3, 2, 1, 4)  1.1 us
  transfers between devices with their start and end apart: 6, of which 5 were waited for; matrix products, arithmetic and copies ran while one was open for 6% of the time, Pallas kernels for 0%

profile of v1, /device:TPU:16, one launch (start us, length us, event | category | flops | bytes accessed | tf_op | source)
XLA Modules:
  0.0 29.2 jit_solution(14484976727946573450)
XLA Ops:
  0.6 0.0 copy-start
  0.6 1.1 %fusion.3 = (bf16[1,16,2,8,128]{4,1,2,3,0:T(8,128)(2,1)S(1)}, bf16[1,16,2,8,128]{4,1,2,3,0:T(8,128)(2,1)S(1)}) fusion(s32[16,2,8,128]{3,2,1,0:T(8,128)} %param.6, bf16[16,2,8,128]{3,2,1,0:T(8,128)(2,1)} %param.5, bf16[16,2,8,128]{3,2,1,0:T(8,128)(2,1)} %param.4), kind=kLoop, calls=%fused_computation.13 | loop fusion | flops 65536 | bytes 393216 | tf_op jit(solution)/shard_map/stack | solution.py:129
  1.8 0.0 copy-start.1
  1.8 1.6 %collective-permute-start = (bf16[2,8,2,16,128]{4,3,2,1,0:T(8,128)(2,1)S(1)}, bf16[2,8,2,16,128]{4,3,2,1,0:T(8,128)(2,1)S(1)}, u32[]{:S(2)}, u32[]{:S(2)}) collective-permute-start(bf16[2,8,2,16,128]{4,3,2,1,0:T(8,128)(2,1)S(1)} %get-tuple-element.13.refs_0_), channel_id=1, source_target_pairs={{0,8},{4,12},{8,0},{12,4},{16,24},{20,28},{24,16},{28,20},{1,9},{5... | collective-permute-start | bytes 393224 | tf_op jit(solution)/shard_map/ppermute | solution.py:132
  3.3 1.5 %collective-permute-start.1 = (bf16[2,8,2,16,128]{4,3,2,1,0:T(8,128)(2,1)S(1)}, bf16[2,8,2,16,128]{4,3,2,1,0:T(8,128)(2,1)S(1)}, u32[]{:S(2)}, u32[]{:S(2)}) collective-permute-start(bf16[2,8,2,16,128]{4,3,2,1,0:T(8,128)(2,1)S(1)} %get-tuple-element.13.refs_0_), channel_id=1, source_target_pairs={{0,16},{4,20},{8,24},{12,28},{16,0},{20,4},{24,8},{28,12},{1,17},{... | collective-permute-start | bytes 393224 | tf_op jit(solution)/shard_map/ppermute | solution.py:132
  4.9 0.5 %collective-permute-start.2 = (bf16[2,8,2,16,128]{4,3,2,1,0:T(8,128)(2,1)S(1)}, bf16[2,8,2,16,128]{4,3,2,1,0:T(8,128)(2,1)S(1)}, u32[]{:S(2)}, u32[]{:S(2)}) collective-permute-start(bf16[2,8,2,16,128]{4,3,2,1,0:T(8,128)(2,1)S(1)} %get-tuple-element.13.refs_0_), channel_id=1, source_target_pairs={{0,24},{4,28},{8,16},{12,20},{16,8},{20,12},{24,0},{28,4},{1,25},{... | collective-permute-start | bytes 393224 | tf_op jit(solution)/shard_map/ppermute | solution.py:132
  5.3 2.2 %collective-permute-done.refs_1_ = bf16[2,8,2,16,128]{4,3,2,1,0:T(8,128)(2,1)S(1)} collective-permute-done((bf16[2,8,2,16,128]{4,3,2,1,0:T(8,128)(2,1)S(1)}, bf16[2,8,2,16,128]{4,3,2,1,0:T(8,128)(2,1)S(1)}, u32[]{:S(2)}, u32[]{:S(2)}) %collective-permute-start) | collective-permute-done | bytes 131104 | tf_op jit(solution)/shard_map/ppermute | solution.py:132
  7.5 0.0 copy-start.2
  7.5 3.6 %collective-permute-done.1.refs_2_ = bf16[2,8,2,16,128]{4,3,2,1,0:T(8,128)(2,1)S(1)} collective-permute-done((bf16[2,8,2,16,128]{4,3,2,1,0:T(8,128)(2,1)S(1)}, bf16[2,8,2,16,128]{4,3,2,1,0:T(8,128)(2,1)S(1)}, u32[]{:S(2)}, u32[]{:S(2)}) %collective-permute-start.1) | collective-permute-done | bytes 131104 | tf_op jit(solution)/shard_map/ppermute | solution.py:132
  11.1 0.0 copy-start.3
  11.1 0.0 collective-permute-done.2.refs_3_
  11.1 0.0 copy-start.4
  11.1 0.1 pad_maximum_fusion
  11.2 0.0 copy-done.1
  11.2 0.0 copy-done.2
  11.2 0.6 %copy-done.3 = bf16[2,8,2,16,128]{4,3,2,1,0:T(8,128)(2,1)} copy-done((bf16[2,8,2,16,128]{4,3,2,1,0:T(8,128)(2,1)}, bf16[2,8,2,16,128]{4,3,2,1,0:T(8,128)(2,1)S(1)}, u32[]{:S(2)}) %copy-start.3) | copy-done | bytes 131096
  11.8 0.1 copy-done.4
  11.8 0.0 collective-permute-start.3
  11.8 0.0 copy-done
  11.8 0.3 %constant_dynamic-slice_fusion = bf16[3,3,3,128,16]{4,3,2,1,0:T(8,128)(2,1)S(1)} fusion(bf16[3,3,3,128,128]{4,3,2,1,0:T(8,128)(2,1)S(1)} %copy-done, s32[]{:T(128)S(6)} %select_n.9), kind=kLoop, calls=%fused_computation.15 | loop fusion | bytes 221188 | tf_op jit(solution)/shard_map/dynamic_slice | solution.py:142
  12.2 0.3 copy.21
  12.5 0.1 copy.20
  12.7 0.9 %reshape.7.refs_8_ = bf16[2,144,384]{2,1,0:T(8,128)(2,1)} reshape(bf16[2,3,3,16,3,128]{5,4,3,2,1,0:T(4,128)(2,1)S(1)} %copy.20) | data formatting | bytes 442368 | tf_op jit(solution)/shard_map/reshape | solution.py:144
  13.5 0.2 collective-permute-done.3
  13.7 0.8 %slice_bitcast_fusion = (bf16[2,8,2,16,128]{4,3,2,1,0:T(8,128)(2,1)}, bf16[2,8,2,16,128]{4,3,2,1,0:T(8,128)(2,1)}, bf16[2,8,2,16,128]{4,3,2,1,0:T(8,128)(2,1)}, bf16[2,8,2,16,128]{4,3,2,1,0:T(8,128)(2,1)}) fusion(bf16[4,2,8,2,16,128]{5,4,3,2,1,0:T(8,128)(2,1)S(1)} %collective-permute-done.3), kind=kLoop, calls=%fused_computation.2 | loop fusion | bytes 1048576 | tf_op jit(solution)/shard_map/squeeze | solution.py:138
  14.5 3.2 %conv.1 = (f32[2,8,16,128]{3,2,1,0:T(8,128)}, f32[2,8,16,128]{3,2,1,0:T(8,128)}, f32[2,8,2,16,128]{4,3,2,1,0:T(8,128)}) custom-call(bf16[2,8,2,16,128]{4,3,2,1,0:T(8,128)(2,1)} %copy-done.1, bf16[2,8,2,16,128]{4,3,2,1,0:T(8,128)(2,1)} %copy-done.2, bf16[2,8,2,16,128]{4,3,2,1,0:T(8,128)(2,1)} %copy-done.3, bf16[2,8,2,16,128]{4,3,2,1,0:T(8,128)(2,1)} %copy-done.4, ...), custom_call_target="tpu_custom_call" | custom-call | tf_op jit(solution)/shard_map/conv/pallas_call | solution.py:147
  17.7 1.6 %collective-permute-start.4 = (f32[2,8,16,128]{3,2,1,0:T(8,128)}, f32[2,8,16,128]{3,2,1,0:T(8,128)S(1)}, u32[]{:S(2)}, u32[]{:S(2)}) collective-permute-start(f32[2,8,16,128]{3,2,1,0:T(8,128)} %get-tuple-element.6), channel_id=1, source_target_pairs={{0,1},{2,3},{1,0},{3,2},{4,5},{6,7},{5,4},{7,6},{8,9},{10,11},{9,8... | collective-permute-start | bytes 393224 | tf_op jit(solution)/shard_map/ppermute | solution.py:159
  19.3 1.9 %collective-permute-start.5 = (f32[2,8,16,128]{3,2,1,0:T(8,128)}, f32[2,8,16,128]{3,2,1,0:T(8,128)S(1)}, u32[]{:S(2)}, u32[]{:S(2)}) collective-permute-start(f32[2,8,16,128]{3,2,1,0:T(8,128)} %get-tuple-element.7), channel_id=1, source_target_pairs={{1,2},{2,1},{5,6},{6,5},{9,10},{10,9},{13,14},{14,13},{17,18},{18,... | collective-permute-start | bytes 393224 | tf_op jit(solution)/shard_map/ppermute | solution.py:159
  21.2 2.4 %collective-permute-done.4.even_ref = f32[2,8,16,128]{3,2,1,0:T(8,128)S(1)} collective-permute-done((f32[2,8,16,128]{3,2,1,0:T(8,128)}, f32[2,8,16,128]{3,2,1,0:T(8,128)S(1)}, u32[]{:S(2)}, u32[]{:S(2)}) %collective-permute-start.4) | collective-permute-done | bytes 131104 | tf_op jit(solution)/shard_map/ppermute | solution.py:159
  23.6 0.0 copy-start.5
  23.7 3.2 %collective-permute-done.5.odd_ref = f32[2,8,16,128]{3,2,1,0:T(8,128)S(1)} collective-permute-done((f32[2,8,16,128]{3,2,1,0:T(8,128)}, f32[2,8,16,128]{3,2,1,0:T(8,128)S(1)}, u32[]{:S(2)}, u32[]{:S(2)}) %collective-permute-start.5) | collective-permute-done | bytes 131104 | tf_op jit(solution)/shard_map/ppermute | solution.py:159
  26.8 0.0 copy-start.6
  26.8 0.0 copy-done.5
  26.8 0.6 %copy-done.6 = f32[2,8,16,128]{3,2,1,0:T(8,128)} copy-done((f32[2,8,16,128]{3,2,1,0:T(8,128)}, f32[2,8,16,128]{3,2,1,0:T(8,128)S(1)}, u32[]{:S(2)}) %copy-start.6) | copy-done | bytes 131096
  27.5 1.8 %add.6 = (bf16[16,2,8,128]{3,2,1,0:T(8,128)(2,1)}, bf16[16,2,8,128]{3,2,1,0:T(8,128)(2,1)}) custom-call(f32[2,8,2,16,128]{4,3,2,1,0:T(8,128)} %get-tuple-element.5.inner_ref, f32[2,8,16,128]{3,2,1,0:T(8,128)} %copy-done.5, f32[2,8,16,128]{3,2,1,0:T(8,128)} %copy-done.6), custom_call_target="tpu_custom_call" | custom-call | tf_op jit(solution)/shard_map/add/pallas_call | solution.py:163
  (4 shorter events, 0.1 us)
Async XLA Ops:
  0.6 11.2 %copy-start = (bf16[3,3,3,128,128]{4,3,2,1,0:T(8,128)(2,1)S(1)}, bf16[3,3,3,128,128]{4,3,2,1,0:T(8,128)(2,1)}, u32[]{:S(2)}) copy-start(bf16[3,3,3,128,128]{4,3,2,1,0:T(8,128)(2,1)} %param.7) | copy-start | bytes 2654212
  1.8 9.4 %copy-start.1 = (bf16[2,8,2,16,128]{4,3,2,1,0:T(8,128)(2,1)}, bf16[2,8,2,16,128]{4,3,2,1,0:T(8,128)(2,1)S(1)}, u32[]{:S(2)}) copy-start(bf16[2,8,2,16,128]{4,3,2,1,0:T(8,128)(2,1)S(1)} %get-tuple-element.13.refs_0_) | copy-start | bytes 393220
  1.8 5.7 %collective-permute-start = (bf16[2,8,2,16,128]{4,3,2,1,0:T(8,128)(2,1)S(1)}, bf16[2,8,2,16,128]{4,3,2,1,0:T(8,128)(2,1)S(1)}, u32[]{:S(2)}, u32[]{:S(2)}) collective-permute-start(bf16[2,8,2,16,128]{4,3,2,1,0:T(8,128)(2,1)S(1)} %get-tuple-element.13.refs_0_), channel_id=1, source_target_pairs={{0,8},{4,12},{8,0},{12,4},{16,24},{20,28},{24,16},{28,20},{1,9},{5... | collective-permute-start | bytes 393224 | tf_op jit(solution)/shard_map/ppermute | solution.py:132
  3.3 7.8 %collective-permute-start.1 = (bf16[2,8,2,16,128]{4,3,2,1,0:T(8,128)(2,1)S(1)}, bf16[2,8,2,16,128]{4,3,2,1,0:T(8,128)(2,1)S(1)}, u32[]{:S(2)}, u32[]{:S(2)}) collective-permute-start(bf16[2,8,2,16,128]{4,3,2,1,0:T(8,128)(2,1)S(1)} %get-tuple-element.13.refs_0_), channel_id=1, source_target_pairs={{0,16},{4,20},{8,24},{12,28},{16,0},{20,4},{24,8},{28,12},{1,17},{... | collective-permute-start | bytes 393224 | tf_op jit(solution)/shard_map/ppermute | solution.py:132
  4.9 6.3 %collective-permute-start.2 = (bf16[2,8,2,16,128]{4,3,2,1,0:T(8,128)(2,1)S(1)}, bf16[2,8,2,16,128]{4,3,2,1,0:T(8,128)(2,1)S(1)}, u32[]{:S(2)}, u32[]{:S(2)}) collective-permute-start(bf16[2,8,2,16,128]{4,3,2,1,0:T(8,128)(2,1)S(1)} %get-tuple-element.13.refs_0_), channel_id=1, source_target_pairs={{0,24},{4,28},{8,16},{12,20},{16,8},{20,12},{24,0},{28,4},{1,25},{... | collective-permute-start | bytes 393224 | tf_op jit(solution)/shard_map/ppermute | solution.py:132
  7.5 3.7 %copy-start.2 = (bf16[2,8,2,16,128]{4,3,2,1,0:T(8,128)(2,1)}, bf16[2,8,2,16,128]{4,3,2,1,0:T(8,128)(2,1)S(1)}, u32[]{:S(2)}) copy-start(bf16[2,8,2,16,128]{4,3,2,1,0:T(8,128)(2,1)S(1)} %collective-permute-done.refs_1_) | copy-start | bytes 393220
  11.1 0.7 %copy-start.3 = (bf16[2,8,2,16,128]{4,3,2,1,0:T(8,128)(2,1)}, bf16[2,8,2,16,128]{4,3,2,1,0:T(8,128)(2,1)S(1)}, u32[]{:S(2)}) copy-start(bf16[2,8,2,16,128]{4,3,2,1,0:T(8,128)(2,1)S(1)} %collective-permute-done.1.refs_2_) | copy-start | bytes 393220
  11.1 0.7 %copy-start.4 = (bf16[2,8,2,16,128]{4,3,2,1,0:T(8,128)(2,1)}, bf16[2,8,2,16,128]{4,3,2,1,0:T(8,128)(2,1)S(1)}, u32[]{:S(2)}) copy-start(bf16[2,8,2,16,128]{4,3,2,1,0:T(8,128)(2,1)S(1)} %collective-permute-done.2.refs_3_) | copy-start | bytes 393220
  11.8 1.9 %collective-permute-start.3 = (bf16[4,2,8,2,16,128]{5,4,3,2,1,0:T(8,128)(2,1)S(1)}, bf16[4,2,8,2,16,128]{5,4,3,2,1,0:T(8,128)(2,1)S(1)}, u32[]{:S(2)}, u32[]{:S(2)}) collective-permute-start(bf16[4,2,8,2,16,128]{5,4,3,2,1,0:T(8,128)(2,1)S(1)} %pad_maximum_fusion), channel_id=1, source_target_pairs={{0,4},{4,0},{8,12},{12,8},{16,20},{20,16},{24,28},{28,24},{1,5},{5... | collective-permute-start | bytes 1572872 | tf_op jit(solution)/shard_map/ppermute | solution.py:132
  17.7 5.9 %collective-permute-start.4 = (f32[2,8,16,128]{3,2,1,0:T(8,128)}, f32[2,8,16,128]{3,2,1,0:T(8,128)S(1)}, u32[]{:S(2)}, u32[]{:S(2)}) collective-permute-start(f32[2,8,16,128]{3,2,1,0:T(8,128)} %get-tuple-element.6), channel_id=1, source_target_pairs={{0,1},{2,3},{1,0},{3,2},{4,5},{6,7},{5,4},{7,6},{8,9},{10,11},{9,8... | collective-permute-start | bytes 393224 | tf_op jit(solution)/shard_map/ppermute | solution.py:159
  19.3 7.5 %collective-permute-start.5 = (f32[2,8,16,128]{3,2,1,0:T(8,128)}, f32[2,8,16,128]{3,2,1,0:T(8,128)S(1)}, u32[]{:S(2)}, u32[]{:S(2)}) collective-permute-start(f32[2,8,16,128]{3,2,1,0:T(8,128)} %get-tuple-element.7), channel_id=1, source_target_pairs={{1,2},{2,1},{5,6},{6,5},{9,10},{10,9},{13,14},{14,13},{17,18},{18,... | collective-permute-start | bytes 393224 | tf_op jit(solution)/shard_map/ppermute | solution.py:159
  23.6 3.2 %copy-start.5 = (f32[2,8,16,128]{3,2,1,0:T(8,128)}, f32[2,8,16,128]{3,2,1,0:T(8,128)S(1)}, u32[]{:S(2)}) copy-start(f32[2,8,16,128]{3,2,1,0:T(8,128)S(1)} %collective-permute-done.4.even_ref) | copy-start | bytes 393220
  26.8 0.7 %copy-start.6 = (f32[2,8,16,128]{3,2,1,0:T(8,128)}, f32[2,8,16,128]{3,2,1,0:T(8,128)S(1)}, u32[]{:S(2)}) copy-start(f32[2,8,16,128]{3,2,1,0:T(8,128)S(1)} %collective-permute-done.5.odd_ref) | copy-start | bytes 393220

commit v2 on v1

--- a/solution.py
+++ b/solution.py
@@ -9,6 +9,7 @@
 
 LANES = 128
 TILE = 16
+CONV_VMEM, ADD_VMEM = 8 << 20, 4 << 20
 F32 = jnp.float32
 
 
@@ -133,15 +134,16 @@
 
     far = list(range(2, devices, 2))
     near = [own] + [swap(own, bit) for bit in far]
-    other = swap(jnp.stack(near), 1)
     sources = [0] + far + [1] + [bit + 1 for bit in far]
-    blocks = near + [other[i] for i in range(len(near))]
 
     start = lax.axis_index("chan") * width
     forward = lax.dynamic_slice_in_dim(weights, start, width, 3)
     backward = lax.dynamic_slice_in_dim(weights, start, width, 4)[::-1, ::-1, ::-1].swapaxes(3, 4)
     lhs = jnp.stack([forward, backward]).transpose(0, 1, 3, 4, 2, 5)
     lhs = lhs.reshape(2, 9 * width, 3 * channels)
+
+    near[-1], lhs = lax.optimization_barrier((near[-1], lhs))
+    blocks = near + [swap(value, 1) for value in near]
 
     edge = jax.ShapeDtypeStruct((2, rows, width, cols), F32)
     even, odd, inner = pl.pallas_call(
@@ -150,6 +152,7 @@
         in_specs=[pl.BlockSpec(memory_space=pltpu.VMEM)] * (len(blocks) + 1),
         out_specs=[pl.BlockSpec(memory_space=pltpu.VMEM)] * 3,
         scratch_shapes=[pltpu.VMEM((2, rows + 2, channels, planes * cols), jnp.bfloat16)],
+        compiler_params=pltpu.CompilerParams(vmem_limit_bytes=CONV_VMEM),
         name="conv",
     )(*blocks, lhs)
 
@@ -166,6 +169,7 @@
             in_specs=[pl.BlockSpec(memory_space=pltpu.VMEM)] * 3,
             out_specs=[pl.BlockSpec(memory_space=pltpu.VMEM)] * 2,
             scratch_shapes=[pltpu.VMEM((width * rows, cols), F32)],
+            compiler_params=pltpu.CompilerParams(vmem_limit_bytes=ADD_VMEM),
             name="add",
         )(inner, even, odd)
     )

time: 29.4 us -> 23.3 us (0.79)
  Pallas kernels: 4.94 us -> 1.76 us
  local copies, waits for them, and re-layouts: 3.73 us -> 0.99 us
  waiting for transfers between devices: 11.6 us -> 10.9 us
  starting transfers between devices: 7.04 us -> 7.62 us
    pallas_call x1, Pallas kernels: 3.18 us -> 1.04 us  [aligned_body(): pl.pallas_call(functools.partial(conv_kernel, width, sources), out_shape=...]
    unnamed x15 -> x3, local copies, waits for them, and re-layouts: 1.57 us -> 0.31 us
    pallas_call x1, Pallas kernels: 1.76 us -> 0.72 us  [aligned_body(): pl.pallas_call(add_kernel, out_shape=(out, out), in_specs=[pl.BlockSpec(m...]
    squeeze x1 -> x0, local copies, waits for them, and re-layouts: 0.81 us -> none  [aligned_body(): blocks = near + [other[i] for i in range(len(near))]]
    reshape x1, local copies, waits for them, and re-layouts: 0.87 us -> 0.19 us  [aligned_body(): lhs = lhs.reshape(2, 9 * width, 3 * channels)]
    ppermute x4 -> x7, starting transfers between devices: 3.56 us -> 4.07 us  [swap(): return lax.ppermute(value, 'chan', [(i, i ^ bit) for i in range(devices)])]
    ppermute x4 -> x7, waiting for transfers between devices: 5.98 us -> 5.47 us  [swap(): return lax.ppermute(value, 'chan', [(i, i ^ bit) for i in range(devices)])]
  transfers between devices with their start and end apart: 6 -> 9, of which waited for: 5 -> 6; matrix products, arithmetic and copies ran while one was open for 6% -> 4% of each run, Pallas kernels for 0% -> 0%
where the time goes in v2:
time: 23.3 us; the launch traced here: 23.1 us
  waiting for transfers between devices  10.9 us (47%)
  starting transfers between devices  7.62 us (33%)
  Pallas kernels  1.76 us (8%)
  other arithmetic  1.14 us (5%)
  local copies, waits for them, and re-layouts  0.99 us (4%)
  between operations  0.72 us (3%)
    ppermute x7, waiting for transfers between devices, swap(): return lax.ppermute(value, 'chan', [(i, i ^ bit) for i in range(devices)])  5.47 us
    ppermute x2, waiting for transfers between devices, aligned_body(): lax.ppermute(v, 'slab', pairs + [(j, i) for i, j in pairs])  5.41 us
    ppermute x7, starting transfers between devices, swap(): return lax.ppermute(value, 'chan', [(i, i ^ bit) for i in range(devices)])  4.07 us
    ppermute x2, starting transfers between devices, aligned_body(): lax.ppermute(v, 'slab', pairs + [(j, i) for i, j in pairs])  3.55 us
    another operation x1, other arithmetic, aligned_body(): own = jnp.stack([activations, masked]).transpose(0, 3, 2, 1, 4)  1.1 us
    pallas_call x1, Pallas kernels, aligned_body(): pl.pallas_call(functools.partial(conv_kernel, width, sources), out_shape=...  1.04 us
    pallas_call x1, Pallas kernels, aligned_body(): pl.pallas_call(add_kernel, out_shape=(out, out), in_specs=[pl.BlockSpec(m...  0.72 us
  transfers between devices with their start and end apart: 9, of which 6 were waited for; matrix products, arithmetic and copies ran while one was open for 4% of the time, Pallas kernels for 0%

profile of v2, /device:TPU:16, one launch (start us, length us, event | category | flops | bytes accessed | tf_op | source)
XLA Modules:
  0.0 23.1 jit_solution(6518349534744820948)
XLA Ops:
  0.6 0.0 copy-start
  0.6 1.1 %fusion.1 = (bf16[1,16,2,8,128]{4,1,2,3,0:T(8,128)(2,1)S(1)}, bf16[1,16,2,8,128]{4,1,2,3,0:T(8,128)(2,1)S(1)}) fusion(s32[16,2,8,128]{3,2,1,0:T(8,128)} %param.6, bf16[16,2,8,128]{3,2,1,0:T(8,128)(2,1)} %param.5, bf16[16,2,8,128]{3,2,1,0:T(8,128)(2,1)} %param.4), kind=kLoop, calls=%fused_computation.6 | loop fusion | flops 65536 | bytes 393216 | tf_op jit(solution)/shard_map/stack | solution.py:130
  1.8 2.5 %collective-permute-start.2 = (bf16[2,8,2,16,128]{4,3,2,1,0:T(8,128)(2,1)S(1)}, bf16[2,8,2,16,128]{4,3,2,1,0:T(8,128)(2,1)S(1)}, u32[]{:S(2)}, u32[]{:S(2)}) collective-permute-start(bf16[2,8,2,16,128]{4,3,2,1,0:T(8,128)(2,1)S(1)} %maximum_bitcast_fusion.1.refs_0_), channel_id=1, source_target_pairs={{0,24},{4,28},{8,16},{12,20},{16,8},{20,12},{24,0},{28,4},{1,25},{... | collective-permute-start | bytes 393224 | tf_op jit(solution)/shard_map/ppermute | solution.py:133
  4.3 0.5 %collective-permute-start = (bf16[2,8,2,16,128]{4,3,2,1,0:T(8,128)(2,1)S(1)}, bf16[2,8,2,16,128]{4,3,2,1,0:T(8,128)(2,1)S(1)}, u32[]{:S(2)}, u32[]{:S(2)}) collective-permute-start(bf16[2,8,2,16,128]{4,3,2,1,0:T(8,128)(2,1)S(1)} %maximum_bitcast_fusion.1.refs_0_), channel_id=1, source_target_pairs={{0,8},{4,12},{8,0},{12,4},{16,24},{20,28},{24,16},{28,20},{1,9},{5... | collective-permute-start | bytes 393224 | tf_op jit(solution)/shard_map/ppermute | solution.py:133
  4.8 0.5 %collective-permute-start.1 = (bf16[2,8,2,16,128]{4,3,2,1,0:T(8,128)(2,1)S(1)}, bf16[2,8,2,16,128]{4,3,2,1,0:T(8,128)(2,1)S(1)}, u32[]{:S(2)}, u32[]{:S(2)}) collective-permute-start(bf16[2,8,2,16,128]{4,3,2,1,0:T(8,128)(2,1)S(1)} %maximum_bitcast_fusion.1.refs_0_), channel_id=1, source_target_pairs={{0,16},{4,20},{8,24},{12,28},{16,0},{20,4},{24,8},{28,12},{1,17},{... | collective-permute-start | bytes 393224 | tf_op jit(solution)/shard_map/ppermute | solution.py:133
  5.3 0.0 collective-permute-start.3
  5.3 0.0 copy-done
  5.3 0.3 %constant_dynamic-slice_fusion = bf16[3,3,3,128,16]{4,3,2,1,0:T(8,128)(2,1)S(1)} fusion(bf16[3,3,3,128,128]{4,3,2,1,0:T(8,128)(2,1)S(1)} %copy-done, s32[]{:T(128)S(6)} %select_n.9), kind=kLoop, calls=%fused_computation.8 | loop fusion | bytes 221188 | tf_op jit(solution)/shard_map/dynamic_slice | solution.py:141
  5.7 0.3 %copy.21 = bf16[3,3,3,128,16]{3,4,2,1,0:T(8,128)(2,1)S(1)} copy(bf16[3,3,3,128,16]{4,3,2,1,0:T(8,128)(2,1)S(1)} %constant_dynamic-slice_fusion) | data formatting | bytes 221184
  6.0 0.1 copy.20
  6.2 0.2 reshape.7.refs_8_
  6.4 2.7 %collective-permute-done.2.refs_3_ = bf16[2,8,2,16,128]{4,3,2,1,0:T(8,128)(2,1)S(1)} collective-permute-done((bf16[2,8,2,16,128]{4,3,2,1,0:T(8,128)(2,1)S(1)}, bf16[2,8,2,16,128]{4,3,2,1,0:T(8,128)(2,1)S(1)}, u32[]{:S(2)}, u32[]{:S(2)}) %collective-permute-start.2) | collective-permute-done | bytes 131104 | tf_op jit(solution)/shard_map/ppermute | solution.py:133
  9.1 0.0 collective-permute-start.6
  9.1 1.7 %collective-permute-done.refs_1_ = bf16[2,8,2,16,128]{4,3,2,1,0:T(8,128)(2,1)S(1)} collective-permute-done((bf16[2,8,2,16,128]{4,3,2,1,0:T(8,128)(2,1)S(1)}, bf16[2,8,2,16,128]{4,3,2,1,0:T(8,128)(2,1)S(1)}, u32[]{:S(2)}, u32[]{:S(2)}) %collective-permute-start) | collective-permute-done | bytes 131104 | tf_op jit(solution)/shard_map/ppermute | solution.py:133
  10.8 0.0 collective-permute-start.4
  10.8 0.0 collective-permute-done.1.refs_2_
  10.8 0.5 %collective-permute-start.5 = (bf16[2,8,2,16,128]{4,3,2,1,0:T(8,128)(2,1)S(1)}, bf16[2,8,2,16,128]{4,3,2,1,0:T(8,128)(2,1)S(1)}, u32[]{:S(2)}, u32[]{:S(2)}) collective-permute-start(bf16[2,8,2,16,128]{4,3,2,1,0:T(8,128)(2,1)S(1)} %collective-permute-done.1.refs_2_), channel_id=1, source_target_pairs={{0,4},{4,0},{8,12},{12,8},{16,20},{20,16},{24,28},{28,24},{1,5},{5... | collective-permute-start | bytes 393224 | tf_op jit(solution)/shard_map/ppermute | solution.py:133
  11.4 0.0 collective-permute-done.3.refs_4_
  11.4 0.0 collective-permute-done.6.refs_7_
  11.4 0.8 %collective-permute-done.4.refs_5_ = bf16[2,8,2,16,128]{4,3,2,1,0:T(8,128)(2,1)S(1)} collective-permute-done((bf16[2,8,2,16,128]{4,3,2,1,0:T(8,128)(2,1)S(1)}, bf16[2,8,2,16,128]{4,3,2,1,0:T(8,128)(2,1)S(1)}, u32[]{:S(2)}, u32[]{:S(2)}) %collective-permute-start.4) | collective-permute-done | bytes 131104 | tf_op jit(solution)/shard_map/ppermute | solution.py:133
  12.2 0.2 collective-permute-done.5.refs_6_
  12.4 1.0 %conv.1 = (f32[2,8,16,128]{3,2,1,0:T(8,128)S(1)}, f32[2,8,16,128]{3,2,1,0:T(8,128)S(1)}, f32[2,8,2,16,128]{4,3,2,1,0:T(8,128)S(1)}) custom-call(bf16[2,8,2,16,128]{4,3,2,1,0:T(8,128)(2,1)S(1)} %maximum_bitcast_fusion.1.refs_0_, bf16[2,8,2,16,128]{4,3,2,1,0:T(8,128)(2,1)S(1)} %collective-permute-done.refs_1_, ...), custom_call_target="tpu_custom_call" | custom-call | tf_op jit(solution)/shard_map/conv/pallas_call | solution.py:149
  13.4 1.6 %collective-permute-start.7 = (f32[2,8,16,128]{3,2,1,0:T(8,128)S(1)}, f32[2,8,16,128]{3,2,1,0:T(8,128)S(1)}, u32[]{:S(2)}, u32[]{:S(2)}) collective-permute-start(f32[2,8,16,128]{3,2,1,0:T(8,128)S(1)} %get-tuple-element.10), channel_id=1, source_target_pairs={{0,1},{2,3},{1,0},{3,2},{4,5},{6,7},{5,4},{7,6},{8,9},{10,11},{9,8... | collective-permute-start | bytes 393224 | tf_op jit(solution)/shard_map/ppermute | solution.py:162
  15.1 1.9 %collective-permute-start.8 = (f32[2,8,16,128]{3,2,1,0:T(8,128)S(1)}, f32[2,8,16,128]{3,2,1,0:T(8,128)S(1)}, u32[]{:S(2)}, u32[]{:S(2)}) collective-permute-start(f32[2,8,16,128]{3,2,1,0:T(8,128)S(1)} %get-tuple-element.11), channel_id=1, source_target_pairs={{1,2},{2,1},{5,6},{6,5},{9,10},{10,9},{13,14},{14,13},{17,18},{18,... | collective-permute-start | bytes 393224 | tf_op jit(solution)/shard_map/ppermute | solution.py:162
  17.0 2.2 %collective-permute-done.7.even_ref = f32[2,8,16,128]{3,2,1,0:T(8,128)S(1)} collective-permute-done((f32[2,8,16,128]{3,2,1,0:T(8,128)S(1)}, f32[2,8,16,128]{3,2,1,0:T(8,128)S(1)}, u32[]{:S(2)}, u32[]{:S(2)}) %collective-permute-start.7) | collective-permute-done | bytes 131104 | tf_op jit(solution)/shard_map/ppermute | solution.py:162
  19.2 3.2 %collective-permute-done.8.odd_ref = f32[2,8,16,128]{3,2,1,0:T(8,128)S(1)} collective-permute-done((f32[2,8,16,128]{3,2,1,0:T(8,128)S(1)}, f32[2,8,16,128]{3,2,1,0:T(8,128)S(1)}, u32[]{:S(2)}, u32[]{:S(2)}) %collective-permute-start.8) | collective-permute-done | bytes 131104 | tf_op jit(solution)/shard_map/ppermute | solution.py:162
  22.4 0.7 %add.6 = (bf16[16,2,8,128]{3,2,1,0:T(8,128)(2,1)}, bf16[16,2,8,128]{3,2,1,0:T(8,128)(2,1)}) custom-call(f32[2,8,2,16,128]{4,3,2,1,0:T(8,128)S(1)} %get-tuple-element.9.inner_ref, f32[2,8,16,128]{3,2,1,0:T(8,128)S(1)} %collective-permute-done.7.even_ref, f32[2,8,16,128]{3,2,1,0:T(8,128)S(1)} %collective-permute-done.8.odd_ref), custom_call_target="tpu_custom_call" | custom-call | tf_op jit(solution)/shard_map/add/pallas_call | solution.py:166
  (4 shorter events, 0.1 us)
Async XLA Ops:
  0.6 4.7 %copy-start = (bf16[3,3,3,128,128]{4,3,2,1,0:T(8,128)(2,1)S(1)}, bf16[3,3,3,128,128]{4,3,2,1,0:T(8,128)(2,1)}, u32[]{:S(2)}) copy-start(bf16[3,3,3,128,128]{4,3,2,1,0:T(8,128)(2,1)} %param.7) | copy-start | bytes 2654212
  1.8 7.3 %collective-permute-start.2 = (bf16[2,8,2,16,128]{4,3,2,1,0:T(8,128)(2,1)S(1)}, bf16[2,8,2,16,128]{4,3,2,1,0:T(8,128)(2,1)S(1)}, u32[]{:S(2)}, u32[]{:S(2)}) collective-permute-start(bf16[2,8,2,16,128]{4,3,2,1,0:T(8,128)(2,1)S(1)} %maximum_bitcast_fusion.1.refs_0_), channel_id=1, source_target_pairs={{0,24},{4,28},{8,16},{12,20},{16,8},{20,12},{24,0},{28,4},{1,25},{... | collective-permute-start | bytes 393224 | tf_op jit(solution)/shard_map/ppermute | solution.py:133
  4.3 6.6 %collective-permute-start = (bf16[2,8,2,16,128]{4,3,2,1,0:T(8,128)(2,1)S(1)}, bf16[2,8,2,16,128]{4,3,2,1,0:T(8,128)(2,1)S(1)}, u32[]{:S(2)}, u32[]{:S(2)}) collective-permute-start(bf16[2,8,2,16,128]{4,3,2,1,0:T(8,128)(2,1)S(1)} %maximum_bitcast_fusion.1.refs_0_), channel_id=1, source_target_pairs={{0,8},{4,12},{8,0},{12,4},{16,24},{20,28},{24,16},{28,20},{1,9},{5... | collective-permute-start | bytes 393224 | tf_op jit(solution)/shard_map/ppermute | solution.py:133
  4.8 6.0 %collective-permute-start.1 = (bf16[2,8,2,16,128]{4,3,2,1,0:T(8,128)(2,1)S(1)}, bf16[2,8,2,16,128]{4,3,2,1,0:T(8,128)(2,1)S(1)}, u32[]{:S(2)}, u32[]{:S(2)}) collective-permute-start(bf16[2,8,2,16,128]{4,3,2,1,0:T(8,128)(2,1)S(1)} %maximum_bitcast_fusion.1.refs_0_), channel_id=1, source_target_pairs={{0,16},{4,20},{8,24},{12,28},{16,0},{20,4},{24,8},{28,12},{1,17},{... | collective-permute-start | bytes 393224 | tf_op jit(solution)/shard_map/ppermute | solution.py:133
  5.3 6.0 %collective-permute-start.3 = (bf16[2,8,2,16,128]{4,3,2,1,0:T(8,128)(2,1)S(1)}, bf16[2,8,2,16,128]{4,3,2,1,0:T(8,128)(2,1)S(1)}, u32[]{:S(2)}, u32[]{:S(2)}) collective-permute-start(bf16[2,8,2,16,128]{4,3,2,1,0:T(8,128)(2,1)S(1)} %maximum_bitcast_fusion.1.refs_0_), channel_id=1, source_target_pairs={{0,4},{4,0},{8,12},{12,8},{16,20},{20,16},{24,28},{28,24},{1,5},{5... | collective-permute-start | bytes 393224 | tf_op jit(solution)/shard_map/ppermute | solution.py:133
  9.1 2.3 %collective-permute-start.6 = (bf16[2,8,2,16,128]{4,3,2,1,0:T(8,128)(2,1)S(1)}, bf16[2,8,2,16,128]{4,3,2,1,0:T(8,128)(2,1)S(1)}, u32[]{:S(2)}, u32[]{:S(2)}) collective-permute-start(bf16[2,8,2,16,128]{4,3,2,1,0:T(8,128)(2,1)S(1)} %collective-permute-done.2.refs_3_), channel_id=1, source_target_pairs={{0,4},{4,0},{8,12},{12,8},{16,20},{20,16},{24,28},{28,24},{1,5},{5... | collective-permute-start | bytes 393224 | tf_op jit(solution)/shard_map/ppermute | solution.py:133
  10.8 1.3 %collective-permute-start.4 = (bf16[2,8,2,16,128]{4,3,2,1,0:T(8,128)(2,1)S(1)}, bf16[2,8,2,16,128]{4,3,2,1,0:T(8,128)(2,1)S(1)}, u32[]{:S(2)}, u32[]{:S(2)}) collective-permute-start(bf16[2,8,2,16,128]{4,3,2,1,0:T(8,128)(2,1)S(1)} %collective-permute-done.refs_1_), channel_id=1, source_target_pairs={{0,4},{4,0},{8,12},{12,8},{16,20},{20,16},{24,28},{28,24},{1,5},{5... | collective-permute-start | bytes 393224 | tf_op jit(solution)/shard_map/ppermute | solution.py:133
  10.8 1.5 %collective-permute-start.5 = (bf16[2,8,2,16,128]{4,3,2,1,0:T(8,128)(2,1)S(1)}, bf16[2,8,2,16,128]{4,3,2,1,0:T(8,128)(2,1)S(1)}, u32[]{:S(2)}, u32[]{:S(2)}) collective-permute-start(bf16[2,8,2,16,128]{4,3,2,1,0:T(8,128)(2,1)S(1)} %collective-permute-done.1.refs_2_), channel_id=1, source_target_pairs={{0,4},{4,0},{8,12},{12,8},{16,20},{20,16},{24,28},{28,24},{1,5},{5... | collective-permute-start | bytes 393224 | tf_op jit(solution)/shard_map/ppermute | solution.py:133
  13.4 5.8 %collective-permute-start.7 = (f32[2,8,16,128]{3,2,1,0:T(8,128)S(1)}, f32[2,8,16,128]{3,2,1,0:T(8,128)S(1)}, u32[]{:S(2)}, u32[]{:S(2)}) collective-permute-start(f32[2,8,16,128]{3,2,1,0:T(8,128)S(1)} %get-tuple-element.10), channel_id=1, source_target_pairs={{0,1},{2,3},{1,0},{3,2},{4,5},{6,7},{5,4},{7,6},{8,9},{10,11},{9,8... | collective-permute-start | bytes 393224 | tf_op jit(solution)/shard_map/ppermute | solution.py:162
  15.1 7.3 %collective-permute-start.8 = (f32[2,8,16,128]{3,2,1,0:T(8,128)S(1)}, f32[2,8,16,128]{3,2,1,0:T(8,128)S(1)}, u32[]{:S(2)}, u32[]{:S(2)}) collective-permute-start(f32[2,8,16,128]{3,2,1,0:T(8,128)S(1)} %get-tuple-element.11), channel_id=1, source_target_pairs={{1,2},{2,1},{5,6},{6,5},{9,10},{10,9},{13,14},{14,13},{17,18},{18,... | collective-permute-start | bytes 393224 | tf_op jit(solution)/shard_map/ppermute | solution.py:162

commit v3 on v2

--- a/solution.py
+++ b/solution.py
@@ -1,4 +1,5 @@
 import functools
+import math
 
 import jax
 import jax.numpy as jnp
@@ -7,8 +8,10 @@
 from jax.experimental.pallas import tpu as pltpu
 from jax.sharding import PartitionSpec as P
 
+
 LANES = 128
 TILE = 16
+INPUT_MAX, WEIGHT_MAX = 6.0, 0.109375
 CONV_VMEM, ADD_VMEM = 8 << 20, 4 << 20
 F32 = jnp.float32
 
@@ -108,16 +111,18 @@
 
 
 def add_kernel(inner_ref, even_ref, odd_ref, pre_ref, grad_ref, turned_ref):
-    arrays, rows, planes, width, cols = inner_ref.shape
-    even = lax.rem(lax.axis_index("slab"), 2) == 0
+    _, rows, planes, width, cols = inner_ref.shape
+    slab = lax.axis_index("slab")
+    even = lax.rem(slab, 2) == 0
+    below, above = slab > 0, slab < lax.axis_size("slab") - 1
     for a, out_ref in enumerate((pre_ref, grad_ref)):
         for p in range(planes):
             for r in range(rows):
                 value = inner_ref[a, r, p]
                 if p == 0:
-                    value = value + jnp.where(even, odd_ref[a, r], even_ref[a, r])
+                    value = value + jnp.where(below, jnp.where(even, odd_ref[a, r], even_ref[a, r]), 0.0)
                 if p == planes - 1:
-                    value = value + jnp.where(even, even_ref[a, r], odd_ref[a, r])
+                    value = value + jnp.where(above, jnp.where(even, even_ref[a, r], odd_ref[a, r]), 0.0)
                 turned_ref[pl.ds(r, width, stride=rows), :] = value
             out_ref[:, p] = turned_ref[...].reshape(width, rows, cols).astype(jnp.bfloat16)
 
@@ -156,11 +161,23 @@
         name="conv",
     )(*blocks, lhs)
 
-    evens = [(i, i + 1) for i in range(0, slabs - 1, 2)]
-    odds = [(i, i + 1) for i in range(1, slabs - 1, 2)]
-    even, odd = (
-        lax.ppermute(v, "slab", pairs + [(j, i) for i, j in pairs]) for v, pairs in ((even, evens), (odd, odds))
-    )
+    largest = 9 * channels * INPUT_MAX * WEIGHT_MAX
+    scale = 2.0 ** math.floor(math.log2(float(jnp.finfo(jnp.float16).max) / largest))
+
+    def exchange(value, first):
+        partner = {}
+        for i in range(first, slabs - 1, 2):
+            partner[i], partner[i + 1] = i + 1, i
+        pairs = [
+            (c * slabs + s, c * slabs + partner[s] if s in partner else (c ^ 1) * slabs + s)
+            for c in range(devices)
+            for s in range(slabs)
+        ]
+        value = (value * scale).astype(jnp.float16)
+        value = lax.ppermute(value, ("chan", "slab"), pairs)
+        return value.astype(F32) * (1 / scale)
+
+    even, odd = exchange(even, 0), exchange(odd, 1)
     out = jax.ShapeDtypeStruct(activations.shape, jnp.bfloat16)
     return tuple(
         pl.pallas_call(
@@ -187,7 +204,9 @@
         and rows % 8 == 0
         and lax.axis_size("slab") > 1
     )
-    return (aligned_body if aligned else general_body)(activations, cotangent, relu_mask, weights)
+    if not aligned:
+        return general_body(activations, cotangent, relu_mask, weights)
+    return aligned_body(activations, cotangent, relu_mask, weights)
 
 
 def solution(mesh):

time: 23.3 us -> 21.4 us (0.918)
  the two profiles are of different devices: /device:TPU:16 before, /device:TPU:0 now
where the time goes in v3:
time: 21.4 us; the launch traced here: 21.3 us
  starting transfers between devices  8.43 us (39%)
  waiting for transfers between devices  8.16 us (38%)
  Pallas kernels  1.77 us (8%)
  other arithmetic  1.2 us (6%)
  local copies, waits for them, and re-layouts  0.99 us (5%)
  between operations  0.73 us (3%)
    ppermute x7, waiting for transfers between devices, swap(): return lax.ppermute(value, 'chan', [(i, i ^ bit) for i in range(devices)])  5.87 us
    ppermute x7, starting transfers between devices, swap(): return lax.ppermute(value, 'chan', [(i, i ^ bit) for i in range(devices)])  5.15 us
    ppermute x2, starting transfers between devices, exchange(): value = lax.ppermute(value, ('chan', 'slab'), pairs)  3.28 us
    ppermute x2, waiting for transfers between devices, exchange(): value = lax.ppermute(value, ('chan', 'slab'), pairs)  2.29 us
    another operation x1, other arithmetic, aligned_body(): own = jnp.stack([activations, masked]).transpose(0, 3, 2, 1, 4)  1.1 us
    pallas_call x1, Pallas kernels, aligned_body(): pl.pallas_call(functools.partial(conv_kernel, width, sources), out_shape=...  1.04 us
    pallas_call x1, Pallas kernels, aligned_body(): pl.pallas_call(add_kernel, out_shape=(out, out), in_specs=[pl.BlockSpec(m...  0.73 us
  transfers between devices with their start and end apart: 9, of which 5 were waited for; matrix products, arithmetic and copies ran while one was open for 5% of the time, Pallas kernels for 0%

profile of v3, /device:TPU:0, one launch (start us, length us, event | category | flops | bytes accessed | tf_op | source)
XLA Modules:
  0.0 21.3 jit_solution(9299448492990081573)
XLA Ops:
  0.6 0.0 copy-start
  0.6 1.1 %fusion.1 = (bf16[1,16,2,8,128]{4,1,2,3,0:T(8,128)(2,1)S(1)}, bf16[1,16,2,8,128]{4,1,2,3,0:T(8,128)(2,1)S(1)}) fusion(s32[16,2,8,128]{3,2,1,0:T(8,128)} %param.6, bf16[16,2,8,128]{3,2,1,0:T(8,128)(2,1)} %param.5, bf16[16,2,8,128]{3,2,1,0:T(8,128)(2,1)} %param.4), kind=kLoop, calls=%fused_computation.10 | loop fusion | flops 65536 | bytes 393216 | tf_op jit(solution)/shard_map/stack | solution.py:135
  1.8 4.0 %collective-permute-start.2 = (bf16[2,8,2,16,128]{4,3,2,1,0:T(8,128)(2,1)S(1)}, bf16[2,8,2,16,128]{4,3,2,1,0:T(8,128)(2,1)S(1)}, u32[]{:S(2)}, u32[]{:S(2)}) collective-permute-start(bf16[2,8,2,16,128]{4,3,2,1,0:T(8,128)(2,1)S(1)} %maximum_bitcast_fusion.1.refs_0_), channel_id=1, source_target_pairs={{0,24},{4,28},{8,16},{12,20},{16,8},{20,12},{24,0},{28,4},{1,25},{... | collective-permute-start | bytes 393224 | tf_op jit(solution)/shard_map/ppermute | solution.py:138
  5.8 0.5 %collective-permute-start = (bf16[2,8,2,16,128]{4,3,2,1,0:T(8,128)(2,1)S(1)}, bf16[2,8,2,16,128]{4,3,2,1,0:T(8,128)(2,1)S(1)}, u32[]{:S(2)}, u32[]{:S(2)}) collective-permute-start(bf16[2,8,2,16,128]{4,3,2,1,0:T(8,128)(2,1)S(1)} %maximum_bitcast_fusion.1.refs_0_), channel_id=1, source_target_pairs={{0,8},{4,12},{8,0},{12,4},{16,24},{20,28},{24,16},{28,20},{1,9},{5... | collective-permute-start | bytes 393224 | tf_op jit(solution)/shard_map/ppermute | solution.py:138
  6.3 0.1 collective-permute-start.1
  6.4 0.0 collective-permute-start.3
  6.4 0.0 copy-done
  6.4 0.3 %constant_dynamic-slice_fusion = bf16[3,3,3,128,16]{4,3,2,1,0:T(8,128)(2,1)S(1)} fusion(bf16[3,3,3,128,128]{4,3,2,1,0:T(8,128)(2,1)S(1)} %copy-done, s32[]{:T(128)S(6)} %select_n.9), kind=kLoop, calls=%fused_computation.12 | loop fusion | bytes 221188 | tf_op jit(solution)/shard_map/dynamic_slice | solution.py:146
  6.8 0.3 %copy.21 = bf16[3,3,3,128,16]{3,4,2,1,0:T(8,128)(2,1)S(1)} copy(bf16[3,3,3,128,16]{4,3,2,1,0:T(8,128)(2,1)S(1)} %constant_dynamic-slice_fusion) | data formatting | bytes 221184
  7.1 0.1 copy.20
  7.3 0.2 reshape.7.refs_8_
  7.5 2.6 %collective-permute-done.2.refs_3_ = bf16[2,8,2,16,128]{4,3,2,1,0:T(8,128)(2,1)S(1)} collective-permute-done((bf16[2,8,2,16,128]{4,3,2,1,0:T(8,128)(2,1)S(1)}, bf16[2,8,2,16,128]{4,3,2,1,0:T(8,128)(2,1)S(1)}, u32[]{:S(2)}, u32[]{:S(2)}) %collective-permute-start.2) | collective-permute-done | bytes 131104 | tf_op jit(solution)/shard_map/ppermute | solution.py:138
  10.1 0.0 collective-permute-start.6
  10.1 2.2 %collective-permute-done.refs_1_ = bf16[2,8,2,16,128]{4,3,2,1,0:T(8,128)(2,1)S(1)} collective-permute-done((bf16[2,8,2,16,128]{4,3,2,1,0:T(8,128)(2,1)S(1)}, bf16[2,8,2,16,128]{4,3,2,1,0:T(8,128)(2,1)S(1)}, u32[]{:S(2)}, u32[]{:S(2)}) %collective-permute-start) | collective-permute-done | bytes 131104 | tf_op jit(solution)/shard_map/ppermute | solution.py:138
  12.3 0.0 collective-permute-start.4
  12.3 0.0 collective-permute-done.1.refs_2_
  12.3 0.5 %collective-permute-start.5 = (bf16[2,8,2,16,128]{4,3,2,1,0:T(8,128)(2,1)S(1)}, bf16[2,8,2,16,128]{4,3,2,1,0:T(8,128)(2,1)S(1)}, u32[]{:S(2)}, u32[]{:S(2)}) collective-permute-start(bf16[2,8,2,16,128]{4,3,2,1,0:T(8,128)(2,1)S(1)} %collective-permute-done.1.refs_2_), channel_id=1, source_target_pairs={{0,4},{4,0},{8,12},{12,8},{16,20},{20,16},{24,28},{28,24},{1,5},{5... | collective-permute-start | bytes 393224 | tf_op jit(solution)/shard_map/ppermute | solution.py:138
  12.8 0.0 collective-permute-done.3.refs_4_
  12.8 0.0 collective-permute-done.6.refs_7_
  12.8 0.8 %collective-permute-done.4.refs_5_ = bf16[2,8,2,16,128]{4,3,2,1,0:T(8,128)(2,1)S(1)} collective-permute-done((bf16[2,8,2,16,128]{4,3,2,1,0:T(8,128)(2,1)S(1)}, bf16[2,8,2,16,128]{4,3,2,1,0:T(8,128)(2,1)S(1)}, u32[]{:S(2)}, u32[]{:S(2)}) %collective-permute-start.4) | collective-permute-done | bytes 131104 | tf_op jit(solution)/shard_map/ppermute | solution.py:138
  13.7 0.2 collective-permute-done.5.refs_6_
  13.8 1.0 %conv.1 = (f32[2,8,16,128]{3,2,1,0:T(8,128)S(1)}, f32[2,8,16,128]{3,2,1,0:T(8,128)S(1)}, f32[2,8,2,16,128]{4,3,2,1,0:T(8,128)S(1)}) custom-call(bf16[2,8,2,16,128]{4,3,2,1,0:T(8,128)(2,1)S(1)} %maximum_bitcast_fusion.1.refs_0_, bf16[2,8,2,16,128]{4,3,2,1,0:T(8,128)(2,1)S(1)} %collective-permute-done.refs_1_, ...), custom_call_target="tpu_custom_call" | custom-call | tf_op jit(solution)/shard_map/conv/pallas_call | solution.py:154
  14.9 0.4 %collective-permute-start.8 = (f16[2,8,16,128]{3,2,1,0:T(8,128)(2,1)S(1)}, f16[2,8,16,128]{3,2,1,0:T(8,128)(2,1)S(1)}, u32[]{:S(2)}, u32[]{:S(2)}) collective-permute-start(f16[2,8,16,128]{3,2,1,0:T(8,128)(2,1)S(1)} %multiply_convert_fusion), channel_id=1, source_target_pairs={{0,4},{1,2},{2,1},{3,7},{4,0},{5,6},{6,5},{7,3},{8,12},{9,10},{10,... | collective-permute-start | bytes 196616 | tf_op jit(solution)/shard_map/ppermute | solution.py:177
  15.3 2.9 %collective-permute-start.7 = (f16[2,8,16,128]{3,2,1,0:T(8,128)(2,1)S(1)}, f16[2,8,16,128]{3,2,1,0:T(8,128)(2,1)S(1)}, u32[]{:S(2)}, u32[]{:S(2)}) collective-permute-start(f16[2,8,16,128]{3,2,1,0:T(8,128)(2,1)S(1)} %multiply_convert_fusion.1), channel_id=1, source_target_pairs={{0,1},{1,0},{2,3},{3,2},{4,5},{5,4},{6,7},{7,6},{8,9},{9,8},{10,11... | collective-permute-start | bytes 196616 | tf_op jit(solution)/shard_map/ppermute | solution.py:177
  18.2 0.0 collective-permute-done.8
  18.2 2.3 %collective-permute-done.7 = f16[2,8,16,128]{3,2,1,0:T(8,128)(2,1)S(1)} collective-permute-done((f16[2,8,16,128]{3,2,1,0:T(8,128)(2,1)S(1)}, f16[2,8,16,128]{3,2,1,0:T(8,128)(2,1)S(1)}, u32[]{:S(2)}, u32[]{:S(2)}) %collective-permute-start.7) | collective-permute-done | bytes 65568 | tf_op jit(solution)/shard_map/ppermute | solution.py:177
  20.5 0.7 %add.6 = (bf16[16,2,8,128]{3,2,1,0:T(8,128)(2,1)}, bf16[16,2,8,128]{3,2,1,0:T(8,128)(2,1)}) custom-call(f32[2,8,2,16,128]{4,3,2,1,0:T(8,128)S(1)} %get-tuple-element.9.inner_ref, f32[2,8,16,128]{3,2,1,0:T(8,128)S(1)} %convert_multiply_fusion.1.even_ref, f32[2,8,16,128]{3,2,1,0:T(8,128)S(1)} %convert_multiply_fusion.odd_ref), custom_call_target="tpu_custom_call" | custom-call | tf_op jit(solution)/shard_map/add/pallas_call | solution.py:183
  (8 shorter events, 0.1 us)
Async XLA Ops:
  0.6 5.8 %copy-start = (bf16[3,3,3,128,128]{4,3,2,1,0:T(8,128)(2,1)S(1)}, bf16[3,3,3,128,128]{4,3,2,1,0:T(8,128)(2,1)}, u32[]{:S(2)}) copy-start(bf16[3,3,3,128,128]{4,3,2,1,0:T(8,128)(2,1)} %param.7) | copy-start | bytes 2654212
  1.8 8.3 %collective-permute-start.2 = (bf16[2,8,2,16,128]{4,3,2,1,0:T(8,128)(2,1)S(1)}, bf16[2,8,2,16,128]{4,3,2,1,0:T(8,128)(2,1)S(1)}, u32[]{:S(2)}, u32[]{:S(2)}) collective-permute-start(bf16[2,8,2,16,128]{4,3,2,1,0:T(8,128)(2,1)S(1)} %maximum_bitcast_fusion.1.refs_0_), channel_id=1, source_target_pairs={{0,24},{4,28},{8,16},{12,20},{16,8},{20,12},{24,0},{28,4},{1,25},{... | collective-permute-start | bytes 393224 | tf_op jit(solution)/shard_map/ppermute | solution.py:138
  5.8 6.6 %collective-permute-start = (bf16[2,8,2,16,128]{4,3,2,1,0:T(8,128)(2,1)S(1)}, bf16[2,8,2,16,128]{4,3,2,1,0:T(8,128)(2,1)S(1)}, u32[]{:S(2)}, u32[]{:S(2)}) collective-permute-start(bf16[2,8,2,16,128]{4,3,2,1,0:T(8,128)(2,1)S(1)} %maximum_bitcast_fusion.1.refs_0_), channel_id=1, source_target_pairs={{0,8},{4,12},{8,0},{12,4},{16,24},{20,28},{24,16},{28,20},{1,9},{5... | collective-permute-start | bytes 393224 | tf_op jit(solution)/shard_map/ppermute | solution.py:138
  6.3 6.0 %collective-permute-start.1 = (bf16[2,8,2,16,128]{4,3,2,1,0:T(8,128)(2,1)S(1)}, bf16[2,8,2,16,128]{4,3,2,1,0:T(8,128)(2,1)S(1)}, u32[]{:S(2)}, u32[]{:S(2)}) collective-permute-start(bf16[2,8,2,16,128]{4,3,2,1,0:T(8,128)(2,1)S(1)} %maximum_bitcast_fusion.1.refs_0_), channel_id=1, source_target_pairs={{0,16},{4,20},{8,24},{12,28},{16,0},{20,4},{24,8},{28,12},{1,17},{... | collective-permute-start | bytes 393224 | tf_op jit(solution)/shard_map/ppermute | solution.py:138
  6.4 6.4 %collective-permute-start.3 = (bf16[2,8,2,16,128]{4,3,2,1,0:T(8,128)(2,1)S(1)}, bf16[2,8,2,16,128]{4,3,2,1,0:T(8,128)(2,1)S(1)}, u32[]{:S(2)}, u32[]{:S(2)}) collective-permute-start(bf16[2,8,2,16,128]{4,3,2,1,0:T(8,128)(2,1)S(1)} %maximum_bitcast_fusion.1.refs_0_), channel_id=1, source_target_pairs={{0,4},{4,0},{8,12},{12,8},{16,20},{20,16},{24,28},{28,24},{1,5},{5... | collective-permute-start | bytes 393224 | tf_op jit(solution)/shard_map/ppermute | solution.py:138
  10.1 2.7 %collective-permute-start.6 = (bf16[2,8,2,16,128]{4,3,2,1,0:T(8,128)(2,1)S(1)}, bf16[2,8,2,16,128]{4,3,2,1,0:T(8,128)(2,1)S(1)}, u32[]{:S(2)}, u32[]{:S(2)}) collective-permute-start(bf16[2,8,2,16,128]{4,3,2,1,0:T(8,128)(2,1)S(1)} %collective-permute-done.2.refs_3_), channel_id=1, source_target_pairs={{0,4},{4,0},{8,12},{12,8},{16,20},{20,16},{24,28},{28,24},{1,5},{5... | collective-permute-start | bytes 393224 | tf_op jit(solution)/shard_map/ppermute | solution.py:138
  12.3 1.3 %collective-permute-start.4 = (bf16[2,8,2,16,128]{4,3,2,1,0:T(8,128)(2,1)S(1)}, bf16[2,8,2,16,128]{4,3,2,1,0:T(8,128)(2,1)S(1)}, u32[]{:S(2)}, u32[]{:S(2)}) collective-permute-start(bf16[2,8,2,16,128]{4,3,2,1,0:T(8,128)(2,1)S(1)} %collective-permute-done.refs_1_), channel_id=1, source_target_pairs={{0,4},{4,0},{8,12},{12,8},{16,20},{20,16},{24,28},{28,24},{1,5},{5... | collective-permute-start | bytes 393224 | tf_op jit(solution)/shard_map/ppermute | solution.py:138
  12.3 1.5 %collective-permute-start.5 = (bf16[2,8,2,16,128]{4,3,2,1,0:T(8,128)(2,1)S(1)}, bf16[2,8,2,16,128]{4,3,2,1,0:T(8,128)(2,1)S(1)}, u32[]{:S(2)}, u32[]{:S(2)}) collective-permute-start(bf16[2,8,2,16,128]{4,3,2,1,0:T(8,128)(2,1)S(1)} %collective-permute-done.1.refs_2_), channel_id=1, source_target_pairs={{0,4},{4,0},{8,12},{12,8},{16,20},{20,16},{24,28},{28,24},{1,5},{5... | collective-permute-start | bytes 393224 | tf_op jit(solution)/shard_map/ppermute | solution.py:138
  14.9 3.3 %collective-permute-start.8 = (f16[2,8,16,128]{3,2,1,0:T(8,128)(2,1)S(1)}, f16[2,8,16,128]{3,2,1,0:T(8,128)(2,1)S(1)}, u32[]{:S(2)}, u32[]{:S(2)}) collective-permute-start(f16[2,8,16,128]{3,2,1,0:T(8,128)(2,1)S(1)} %multiply_convert_fusion), channel_id=1, source_target_pairs={{0,4},{1,2},{2,1},{3,7},{4,0},{5,6},{6,5},{7,3},{8,12},{9,10},{10,... | collective-permute-start | bytes 196616 | tf_op jit(solution)/shard_map/ppermute | solution.py:177
  15.3 5.2 %collective-permute-start.7 = (f16[2,8,16,128]{3,2,1,0:T(8,128)(2,1)S(1)}, f16[2,8,16,128]{3,2,1,0:T(8,128)(2,1)S(1)}, u32[]{:S(2)}, u32[]{:S(2)}) collective-permute-start(f16[2,8,16,128]{3,2,1,0:T(8,128)(2,1)S(1)} %multiply_convert_fusion.1), channel_id=1, source_target_pairs={{0,1},{1,0},{2,3},{3,2},{4,5},{5,4},{6,7},{7,6},{8,9},{9,8},{10,11... | collective-permute-start | bytes 196616 | tf_op jit(solution)/shard_map/ppermute | solution.py:177

commit v4 on v3

v4 whole, which is shorter than its diff:
```python
import functools
import math

import jax
import jax.numpy as jnp
from jax import lax
from jax.experimental import pallas as pl
from jax.experimental.pallas import tpu as pltpu
from jax.sharding import PartitionSpec as P


LANES = 128
TILE = 16
INPUT_MAX, WEIGHT_MAX = 6.0, 0.109375
CONV_VMEM, ADD_VMEM = 8 << 20, 4 << 20
F32 = jnp.float32
ROUNDS = 3


def with_halo(shard, sides, width):
    for axis, dim in sides:
        devices, length = (lax.axis_size(axis), shard.shape[dim])
        up = [(i, (i + 1) % devices) for i in range(devices - 1)]
        down = [(j, i) for i, j in up]
        last = lax.slice_in_dim(shard, length - width, length, axis=dim)
        first = lax.slice_in_dim(shard, 0, width, axis=dim)
        before = lax.ppermute(last, axis, up)
        after = lax.ppermute(first, axis, down)
        shard = jnp.concatenate([before, shard, after], axis=dim)
    return shard


def tap_sum(weights, padded, planes, height, breadth, equation, flipped):
    total = None
    for i in range(3):
        for j in range(3):
            for k in range(3):
                a, b, c = (2 - i, 2 - j, 2 - k) if flipped else (i, j, k)
                window = padded[:, a : a + planes, b : b + height, c : c + breadth]
                term = jnp.einsum(equation, weights[i, j, k], window, preferred_element_type=F32)
                total = term if total is None else total + term
    return total.astype(jnp.bfloat16)


def general_body(activations, cotangent, relu_mask, weights):
    planes, breadth = activations.shape[1], activations.shape[3]
    masked = jnp.where(relu_mask == 1, cotangent, jnp.zeros_like(cotangent))
    stacked = jnp.stack([activations, masked])
    patches = lax.all_to_all(stacked, "chan", split_axis=3, concat_axis=1, tiled=True)
    rimmed = with_halo(patches, (("chan", 3), ("slab", 2)), 1)
    padded = jnp.pad(rimmed, ((0, 0), (0, 0), (0, 0), (0, 0), (1, 1)))
    height = patches.shape[3]
    pre = tap_sum(weights, padded[0], planes, height, breadth, "oi,idhw->odhw", False)
    grad = tap_sum(weights, padded[1], planes, height, breadth, "oi,odhw->idhw", True)
    return tuple(
        lax.all_to_all(block, "chan", split_axis=0, concat_axis=2, tiled=True) for block in (pre, grad)
    )


def window(blocks, a, r, planes):
    sides = []
    for p in planes:
        pieces = []
        for row in (r - 1, r, r + 1):
            inside = 0 <= row < blocks[0].shape[1]
            pieces += [b[a, row, p] if inside else jnp.zeros(b.shape[3:], b.dtype) for b in blocks]
        sides.append(jnp.concatenate(pieces, axis=0))
    return sides[0] if len(sides) == 1 else jnp.concatenate(sides, axis=1)


def columns(taps):
    left, mid, right = taps
    lane = lax.broadcasted_iota(jnp.int32, mid.shape, 1)
    left = jnp.where(lane == 0, 0.0, pltpu.roll(left, 1, 1))
    right = jnp.where(lane == mid.shape[1] - 1, 0.0, pltpu.roll(right, mid.shape[1] - 1, 1))
    return left + mid + right


def all_planes(lhs, blocks, a, r, wanted):
    _, _, planes, width, cols = blocks[0].shape
    y = jnp.dot(lhs, window(blocks, a, r, range(planes)), preferred_element_type=F32)

    def part(t, k, p):
        top = (t * 3 + k) * width
        return y[top : top + width, p * cols : (p + 1) * cols]

    def plane(q):
        inputs = [p for p in range(planes) if 0 <= p - q + 1 <= 2]
        return columns([functools.reduce(jnp.add, [part(p - q + 1, k, p) for p in inputs]) for k in range(3)])

    return [plane(q) for q in wanted]


def early_kernel(count, lhs_ref, *refs):
    blocks, sum_ref = refs[:count], refs[count]
    arrays, rows, planes, width, _ = blocks[0].shape
    depth = 3 * count * width
    for a in range(arrays):
        lhs = lhs_ref[a, :, :depth]
        for r in range(rows):
            for q, value in enumerate(all_planes(lhs, blocks, a, r, range(-1, planes + 1))):
                sum_ref[a, r, q] = value


def edge_kernel(count, start, lhs_ref, sum_ref, *refs):
    blocks, edge_refs = refs[:count], refs[count:]
    arrays, rows, planes, width, _ = blocks[0].shape
    depth = 3 * count * width
    slab = lax.axis_index("slab")

    def edge(a, r, t, p):
        lhs = lhs_ref[a, t * 3 * width : (t + 1) * 3 * width, start : start + depth]
        y = jnp.dot(lhs, window(blocks, a, r, [p]), preferred_element_type=F32)
        return columns([y[k * width : (k + 1) * width] for k in range(3)])

    for a in range(arrays):
        for r in range(rows):
            below = edge(a, r, 2, 0) + sum_ref[a, r, 0]
            above = edge(a, r, 0, planes - 1) + sum_ref[a, r, planes + 1]
            for j, edge_ref in enumerate(edge_refs):
                edge_ref[a, r] = jnp.where(lax.rem(slab, ROUNDS) == j, above, below)


def inner_kernel(count, start, lhs_ref, sum_ref, *refs):
    blocks, inner_ref = refs[:count], refs[count]
    arrays, rows, planes, width, _ = blocks[0].shape
    depth = 3 * count * width
    for a in range(arrays):
        lhs = lhs_ref[a, :, start : start + depth]
        for r in range(rows):
            for p, value in enumerate(all_planes(lhs, blocks, a, r, range(planes))):
                inner_ref[a, r, p] = value + sum_ref[a, r, p + 1]


def add_kernel(inner_ref, *refs):
    edge_refs, (pre_ref, grad_ref, turned_ref) = refs[:ROUNDS], refs[ROUNDS:]
    _, rows, planes, width, cols = inner_ref.shape
    slab = lax.axis_index("slab")
    below, above = slab > 0, slab < lax.axis_size("slab") - 1

    def received(a, r, pair, exists):
        value = edge_refs[0][a, r]
        for j in range(1, ROUNDS):
            value = jnp.where(lax.rem(pair, ROUNDS) == j, edge_refs[j][a, r], value)
        return jnp.where(exists, value, 0.0)

    for a, out_ref in enumerate((pre_ref, grad_ref)):
        for p in range(planes):
            for r in range(rows):
                value = inner_ref[a, r, p]
                if p == 0:
                    value = value + received(a, r, slab + ROUNDS - 1, below)
                if p == planes - 1:
                    value = value + received(a, r, slab, above)
                turned_ref[pl.ds(r, width, stride=rows), :] = value
            out_ref[:, p] = turned_ref[...].reshape(width, rows, cols).astype(jnp.bfloat16)


def aligned_body(activations, cotangent, relu_mask, weights):
    width, planes, rows, cols = activations.shape
    devices, slabs = lax.axis_size("chan"), lax.axis_size("slab")
    channels = width * devices
    masked = jnp.where(relu_mask == 1, cotangent, jnp.zeros_like(cotangent))
    own = jnp.stack([activations, masked]).transpose(0, 3, 2, 1, 4)

    def swap(value, bit):
        return lax.ppermute(value, "chan", [(i, i ^ bit) for i in range(devices)])

    far = list(range(2, devices, 2))
    last = far.pop()
    early = [0, last]
    near = {bit: own if bit == 0 else swap(own, bit) for bit in early + far}

    me = lax.axis_index("chan")
    forward = lax.dynamic_slice_in_dim(weights, me * width, width, 3)
    backward = lax.dynamic_slice_in_dim(weights, me * width, width, 4)[::-1, ::-1, ::-1].swapaxes(3, 4)
    lhs = jnp.stack([forward, backward]).transpose(0, 1, 3, 4, 2, 5)
    lhs = lhs.reshape(2 * 9 * width, 3 * channels)
    column, start = [], 0
    for bits in (early, far):
        start = len(column)
        column += [
            (k, bit, i) for k in range(3) for near_bit in bits for bit in (near_bit, near_bit + 1) for i in range(width)
        ]
        column += [(3, 0, 0)] * (-len(column) % LANES)
    tap, bit, inside = (jnp.array(v, jnp.int32) for v in zip(*column))
    target = tap * channels + jnp.bitwise_xor(bit, me) * width + inside
    target = jnp.where(tap == 3, -1, target)
    order = (lax.broadcasted_iota(jnp.int32, (3 * channels, len(column)), 0) == target[None]).astype(jnp.bfloat16)
    lhs = jnp.dot(lhs, order, preferred_element_type=F32).astype(jnp.bfloat16).reshape(2, 9 * width, len(column))

    near[last], lhs = lax.optimization_barrier((near[last], lhs))
    blocks = {}
    for bit in early + far:
        blocks[bit] = near[bit]
        blocks[bit + 1] = swap(near[bit], 1)
    first = [blocks[bit + i] for bit in early for i in (0, 1)]
    second = [blocks[bit + i] for bit in far for i in (0, 1)]

    def call(kernel, out_shape, *args):
        return pl.pallas_call(
            kernel,
            out_shape=out_shape,
            in_specs=[pl.BlockSpec(memory_space=pltpu.VMEM)] * len(args),
            out_specs=jax.tree.map(lambda _: pl.BlockSpec(memory_space=pltpu.VMEM), out_shape),
            compiler_params=pltpu.CompilerParams(vmem_limit_bytes=CONV_VMEM),
            cost_estimate=pl.CostEstimate(flops=1 << 28, bytes_accessed=1 << 20, transcendentals=0),
        )(*args)

    def sums(*middle):
        return jax.ShapeDtypeStruct((2, rows, *middle, width, cols), F32)

    total = call(functools.partial(early_kernel, len(first)), sums(planes + 2), lhs, *first)
    edges = call(functools.partial(edge_kernel, len(second), start), (sums(),) * ROUNDS, lhs, total, *second)

    largest = 9 * channels * INPUT_MAX * WEIGHT_MAX
    scale = 2.0 ** math.floor(math.log2(float(jnp.finfo(jnp.float16).max) / largest))

    def exchange(value, turn):
        partner = {}
        for i in range(turn, slabs - 1, ROUNDS):
            partner[i], partner[i + 1] = i + 1, i
        pairs = [
            (c * slabs + s, c * slabs + partner[s] if s in partner else (c ^ 1) * slabs + s)
            for c in range(devices)
            for s in range(slabs)
        ]
        value = (value * scale).astype(jnp.float16)
        value = lax.ppermute(value, ("chan", "slab"), pairs)
        return value.astype(F32) * (1 / scale)

    edges = [exchange(value, turn) for turn, value in enumerate(edges)]
    inner = call(functools.partial(inner_kernel, len(second), start), sums(planes), lhs, total, *second)
    out = jax.ShapeDtypeStruct(activations.shape, jnp.bfloat16)
    return tuple(
        pl.pallas_call(
            add_kernel,
            out_shape=(out, out),
            in_specs=[pl.BlockSpec(memory_space=pltpu.VMEM)] * (ROUNDS + 1),
            out_specs=[pl.BlockSpec(memory_space=pltpu.VMEM)] * 2,
            scratch_shapes=[pltpu.VMEM((width * rows, cols), F32)],
            compiler_params=pltpu.CompilerParams(vmem_limit_bytes=ADD_VMEM),
            name="add",
        )(inner, *edges)
    )


def body(activations, cotangent, relu_mask, weights):
    width, planes, rows, cols = activations.shape
    devices = lax.axis_size("chan")
    aligned = (
        width % TILE == 0
        and cols == LANES
        and devices & (devices - 1) == 0
        and devices > 4
        and planes >= 2
        and rows % 8 == 0
        and lax.axis_size("slab") > 1
    )
    if not aligned:
        return general_body(activations, cotangent, relu_mask, weights)
    return aligned_body(activations, cotangent, relu_mask, weights)


def solution(mesh):
    placed = P("chan", "slab", None, None)
    return jax.shard_map(
        body,
        mesh=mesh,
        in_specs=(placed, placed, placed, P()),
        out_specs=(placed, placed),
        check_vma=False,
    )
```

time: 21.4 us -> 22.7 us (1.061)
  waiting for transfers between devices: 8.16 us -> 6.14 us
  starting transfers between devices: 8.43 us -> 10.1 us
  Pallas kernels: 1.77 us -> 2.52 us
  matrix products: 0 us -> 0.37 us
  local copies, waits for them, and re-layouts: 0.99 us -> 1.33 us
    ppermute x2 -> x3, starting transfers between devices: 3.28 us -> 4.92 us  [exchange(): value = lax.ppermute(value, ('chan', 'slab'), pairs)]
    ppermute x7, waiting for transfers between devices: 5.87 us -> 4.5 us  [swap(): return lax.ppermute(value, 'chan', [(i, i ^ bit) for i in range(devices)])]
    pallas_call x1 -> x3, Pallas kernels: 1.04 us -> 1.78 us  [call(): pl.pallas_call(kernel, out_shape=out_shape, in_specs=[pl.BlockSpec(memory...]
    ppermute x2 -> x3, waiting for transfers between devices: 2.29 us -> 1.64 us  [exchange(): value = lax.ppermute(value, ('chan', 'slab'), pairs)]
    unnamed x3 -> x9, local copies, waits for them, and re-layouts: 0.31 us -> 0.85 us
    dot_general x0 -> x1, matrix products: none -> 0.37 us  [aligned_body(): jnp.dot(lhs, order, preferred_element_type=F32).astype(jnp.bfloat16)]
  transfers between devices with their start and end apart: 9 -> 10, of which waited for: 5 -> 5; matrix products, arithmetic and copies ran while one was open for 5% -> 6% of each run, Pallas kernels for 0% -> 5%
where the time goes in v4:
time: 22.7 us; the launch traced here: 22.5 us
  starting transfers between devices  10.1 us (44%)
  waiting for transfers between devices  6.14 us (27%)
  Pallas kernels  2.52 us (11%)
  local copies, waits for them, and re-layouts  1.33 us (6%)
  other arithmetic  1.24 us (5%)
  between operations  0.8 us (4%)
  matrix products  0.37 us (2%)
    ppermute x7, starting transfers between devices, swap(): return lax.ppermute(value, 'chan', [(i, i ^ bit) for i in range(devices)])  5.22 us
    ppermute x3, starting transfers between devices, exchange(): value = lax.ppermute(value, ('chan', 'slab'), pairs)  4.92 us
    ppermute x7, waiting for transfers between devices, swap(): return lax.ppermute(value, 'chan', [(i, i ^ bit) for i in range(devices)])  4.5 us
    pallas_call x3, Pallas kernels, call(): pl.pallas_call(kernel, out_shape=out_shape, in_specs=[pl.BlockSpec(memory...  1.78 us
    ppermute x3, waiting for transfers between devices, exchange(): value = lax.ppermute(value, ('chan', 'slab'), pairs)  1.64 us
    another operation x1, other arithmetic, aligned_body(): own = jnp.stack([activations, masked]).transpose(0, 3, 2, 1, 4)  1.1 us
    unnamed x9, local copies, waits for them, and re-layouts  0.85 us
    pallas_call x1, Pallas kernels, aligned_body(): pl.pallas_call(add_kernel, out_shape=(out, out), in_specs=[pl.BlockSpec(m...  0.74 us
  transfers between devices with their start and end apart: 10, of which 5 were waited for; matrix products, arithmetic and copies ran while one was open for 6% of the time, Pallas kernels for 5%

profile of v4, /device:TPU:0, one launch (start us, length us, event | category | flops | bytes accessed | tf_op | source)
XLA Modules:
  0.0 22.5 jit_solution(1657299804598204901)
XLA Ops:
  0.6 0.0 copy-start
  0.6 1.1 %fusion.4 = (bf16[1,16,2,8,128]{4,1,2,3,0:T(8,128)(2,1)S(1)}, bf16[1,16,2,8,128]{4,1,2,3,0:T(8,128)(2,1)S(1)}) fusion(s32[16,2,8,128]{3,2,1,0:T(8,128)} %param.9, bf16[16,2,8,128]{3,2,1,0:T(8,128)(2,1)} %param.8, bf16[16,2,8,128]{3,2,1,0:T(8,128)(2,1)} %param.7), kind=kLoop, calls=%fused_computation.17 | loop fusion | flops 65536 | bytes 393216 | tf_op jit(solution)/shard_map/stack | solution.py:164
  1.8 4.0 %collective-permute-start = (bf16[2,8,2,16,128]{4,3,2,1,0:T(8,128)(2,1)S(1)}, bf16[2,8,2,16,128]{4,3,2,1,0:T(8,128)(2,1)S(1)}, u32[]{:S(2)}, u32[]{:S(2)}) collective-permute-start(bf16[2,8,2,16,128]{4,3,2,1,0:T(8,128)(2,1)S(1)} %maximum_bitcast_fusion.1.refs_0_), channel_id=1, source_target_pairs={{0,24},{4,28},{8,16},{12,20},{16,8},{20,12},{24,0},{28,4},{1,25},{... | collective-permute-start | bytes 393224 | tf_op jit(solution)/shard_map/ppermute | solution.py:167
  5.8 0.0 collective-permute-start.1
  5.8 0.5 %collective-permute-start.3 = (bf16[2,8,2,16,128]{4,3,2,1,0:T(8,128)(2,1)S(1)}, bf16[2,8,2,16,128]{4,3,2,1,0:T(8,128)(2,1)S(1)}, u32[]{:S(2)}, u32[]{:S(2)}) collective-permute-start(bf16[2,8,2,16,128]{4,3,2,1,0:T(8,128)(2,1)S(1)} %maximum_bitcast_fusion.1.refs_0_), channel_id=1, source_target_pairs={{0,8},{4,12},{8,0},{12,4},{16,24},{20,28},{24,16},{28,20},{1,9},{5... | collective-permute-start | bytes 393224 | tf_op jit(solution)/shard_map/ppermute | solution.py:167
  6.3 0.2 collective-permute-start.5
  6.5 0.0 copy-done
  6.5 0.3 %constant_dynamic-slice_fusion = bf16[3,3,3,128,16]{4,3,2,1,0:T(8,128)(2,1)S(1)} fusion(bf16[3,3,3,128,128]{4,3,2,1,0:T(8,128)(2,1)S(1)} %copy-done, s32[]{:T(128)S(6)} %select_n.13), kind=kLoop, calls=%fused_computation.20 | loop fusion | bytes 221188 | tf_op jit(solution)/shard_map/dynamic_slice | solution.py:176
  6.8 0.3 %copy.23 = bf16[3,3,3,128,16]{3,4,2,1,0:T(8,128)(2,1)S(1)} copy(bf16[3,3,3,128,16]{4,3,2,1,0:T(8,128)(2,1)S(1)} %constant_dynamic-slice_fusion) | data formatting | bytes 221184
  7.2 0.0 copy-start.1
  7.2 0.0 copy-start.2
  7.2 0.0 copy-start.3
  7.2 0.1 copy.22
  7.4 0.5 %copy-done.1 = s32[512]{0:T(512)S(1)} copy-done((s32[512]{0:T(512)S(1)}, s32[512]{0:T(512)}, u32[]{:S(2)}) %copy-start.1) | copy-done | bytes 2072
  7.9 0.0 copy-done.2
  7.9 0.0 copy-done.3
  7.9 0.4 %convolution_convert_fusion = bf16[288,512]{1,0:T(8,128)(2,1)S(1)} fusion(s32[512]{0:T(512)S(1)} %add_select_fusion, bf16[36,8,3,128]{3,2,1,0:T(4,128)(2,1)S(1)} %bitcast.23), kind=kOutput, calls=%fused_computation | convolution fusion | flops 113590272 | bytes 518144 | tf_op jit(solution)/shard_map/dot_general | solution.py:190
  8.3 1.4 %collective-permute-done.refs_2_ = bf16[2,8,2,16,128]{4,3,2,1,0:T(8,128)(2,1)S(1)} collective-permute-done((bf16[2,8,2,16,128]{4,3,2,1,0:T(8,128)(2,1)S(1)}, bf16[2,8,2,16,128]{4,3,2,1,0:T(8,128)(2,1)S(1)}, u32[]{:S(2)}, u32[]{:S(2)}) %collective-permute-start) | collective-permute-done | bytes 131104 | tf_op jit(solution)/shard_map/ppermute | solution.py:167
  9.7 0.0 collective-permute-start.2
  9.7 2.6 %collective-permute-done.3.refs_0_ = bf16[2,8,2,16,128]{4,3,2,1,0:T(8,128)(2,1)S(1)} collective-permute-done((bf16[2,8,2,16,128]{4,3,2,1,0:T(8,128)(2,1)S(1)}, bf16[2,8,2,16,128]{4,3,2,1,0:T(8,128)(2,1)S(1)}, u32[]{:S(2)}, u32[]{:S(2)}) %collective-permute-start.3) | collective-permute-done | bytes 131104 | tf_op jit(solution)/shard_map/ppermute | solution.py:167
  12.3 0.0 collective-permute-start.4
  12.3 0.0 collective-permute-done.5.refs_2_
  12.3 0.5 %collective-permute-start.6 = (bf16[2,8,2,16,128]{4,3,2,1,0:T(8,128)(2,1)S(1)}, bf16[2,8,2,16,128]{4,3,2,1,0:T(8,128)(2,1)S(1)}, u32[]{:S(2)}, u32[]{:S(2)}) collective-permute-start(bf16[2,8,2,16,128]{4,3,2,1,0:T(8,128)(2,1)S(1)} %collective-permute-done.5.refs_2_), channel_id=1, source_target_pairs={{0,4},{4,0},{8,12},{12,8},{16,20},{20,16},{24,28},{28,24},{1,5},{5... | collective-permute-start | bytes 393224 | tf_op jit(solution)/shard_map/ppermute | solution.py:167
  12.8 0.0 collective-permute-done.1.refs_1_
  12.8 0.0 collective-permute-done.2.refs_3_
  12.8 0.5 %shard_map.86.sum_ref = f32[2,8,4,16,128]{4,3,2,1,0:T(8,128)S(1)} custom-call(bf16[2,144,512]{2,1,0:T(8,128)(2,1)S(1)} %bitcast.20, bf16[2,8,2,16,128]{4,3,2,1,0:T(8,128)(2,1)S(1)} %maximum_bitcast_fusion.1.refs_0_, bf16[2,8,2,16,128]{4,3,2,1,0:T(8,128)(2,1)S(1)} %collective-permute-done.1.refs_1_, ...), custom_call_target="tpu_custom_call" | custom-call | flops 268435456 | bytes 1048576 | tf_op jit(solution)/shard_map/pallas_call | solution.py:201
  13.4 0.3 %collective-permute-done.4.refs_1_ = bf16[2,8,2,16,128]{4,3,2,1,0:T(8,128)(2,1)S(1)} collective-permute-done((bf16[2,8,2,16,128]{4,3,2,1,0:T(8,128)(2,1)S(1)}, bf16[2,8,2,16,128]{4,3,2,1,0:T(8,128)(2,1)S(1)}, u32[]{:S(2)}, u32[]{:S(2)}) %collective-permute-start.4) | collective-permute-done | bytes 131104 | tf_op jit(solution)/shard_map/ppermute | solution.py:167
  13.7 0.2 collective-permute-done.6.refs_3_
  13.8 0.7 %shard_map.88 = (f32[2,8,16,128]{3,2,1,0:T(8,128)S(1)}, f32[2,8,16,128]{3,2,1,0:T(8,128)S(1)}, f32[2,8,16,128]{3,2,1,0:T(8,128)S(1)}) custom-call(bf16[2,144,512]{2,1,0:T(8,128)(2,1)S(1)} %bitcast.21, f32[2,8,4,16,128]{4,3,2,1,0:T(8,128)S(1)} %shard_map.86.sum_ref, bf16[2,8,2,16,128]{4,3,2,1,0:T(8,128)(2,1)S(1)} %collective-permute-done.3.refs_0_, ...), custom_call_target="tpu_custom_call" | custom-call | flops 268435456 | bytes 1048576 | tf_op jit(solution)/shard_map/pallas_call | solution.py:201
  14.6 0.4 %collective-permute-start.9 = (f16[2,8,16,128]{3,2,1,0:T(8,128)(2,1)S(1)}, f16[2,8,16,128]{3,2,1,0:T(8,128)(2,1)S(1)}, u32[]{:S(2)}, u32[]{:S(2)}) collective-permute-start(f16[2,8,16,128]{3,2,1,0:T(8,128)(2,1)S(1)} %multiply_convert_fusion), channel_id=1, source_target_pairs={{0,4},{1,5},{2,3},{3,2},{4,0},{5,1},{6,7},{7,6},{8,12},{9,13},{10,... | collective-permute-start | bytes 196616 | tf_op jit(solution)/shard_map/ppermute | solution.py:229
  15.0 0.2 %collective-permute-start.8 = (f16[2,8,16,128]{3,2,1,0:T(8,128)(2,1)S(1)}, f16[2,8,16,128]{3,2,1,0:T(8,128)(2,1)S(1)}, u32[]{:S(2)}, u32[]{:S(2)}) collective-permute-start(f16[2,8,16,128]{3,2,1,0:T(8,128)(2,1)S(1)} %multiply_convert_fusion.1), channel_id=1, source_target_pairs={{0,4},{1,2},{2,1},{3,7},{4,0},{5,6},{6,5},{7,3},{8,12},{9,10},{10,... | collective-permute-start | bytes 196616 | tf_op jit(solution)/shard_map/ppermute | solution.py:229
  15.3 4.3 %collective-permute-start.7 = (f16[2,8,16,128]{3,2,1,0:T(8,128)(2,1)S(1)}, f16[2,8,16,128]{3,2,1,0:T(8,128)(2,1)S(1)}, u32[]{:S(2)}, u32[]{:S(2)}) collective-permute-start(f16[2,8,16,128]{3,2,1,0:T(8,128)(2,1)S(1)} %multiply_convert_fusion.2), channel_id=1, source_target_pairs={{0,1},{1,0},{2,6},{3,7},{4,5},{5,4},{6,2},{7,3},{8,9},{9,8},{10,14... | collective-permute-start | bytes 196616 | tf_op jit(solution)/shard_map/ppermute | solution.py:229
  19.5 0.5 %shard_map.87.inner_ref = f32[2,8,2,16,128]{4,3,2,1,0:T(8,128)S(1)} custom-call(bf16[2,144,512]{2,1,0:T(8,128)(2,1)S(1)} %bitcast.22, f32[2,8,4,16,128]{4,3,2,1,0:T(8,128)S(1)} %shard_map.86.sum_ref, bf16[2,8,2,16,128]{4,3,2,1,0:T(8,128)(2,1)S(1)} %collective-permute-done.3.refs_0_, bf16[2,8,2,16,128]{4,3,2,1,0:T(8,128)(2,1)S(1)} %collective-permute-done.4.refs_1_, ...), custom_call_target="tpu_custom_call" | custom-call | flops 268435456 | bytes 1048576 | tf_op jit(solution)/shard_map/pallas_call | solution.py:201
  20.1 0.0 collective-permute-done.9
  20.1 0.0 collective-permute-done.8
  20.1 1.6 %collective-permute-done.7 = f16[2,8,16,128]{3,2,1,0:T(8,128)(2,1)S(1)} collective-permute-done((f16[2,8,16,128]{3,2,1,0:T(8,128)(2,1)S(1)}, f16[2,8,16,128]{3,2,1,0:T(8,128)(2,1)S(1)}, u32[]{:S(2)}, u32[]{:S(2)}) %collective-permute-start.7) | collective-permute-done | bytes 65568 | tf_op jit(solution)/shard_map/ppermute | solution.py:229
  21.8 0.7 %add.18 = (bf16[16,2,8,128]{3,2,1,0:T(8,128)(2,1)}, bf16[16,2,8,128]{3,2,1,0:T(8,128)(2,1)}) custom-call(f32[2,8,2,16,128]{4,3,2,1,0:T(8,128)S(1)} %shard_map.87.inner_ref, f32[2,8,16,128]{3,2,1,0:T(8,128)S(1)} %convert_multiply_fusion.2.refs_0_, f32[2,8,16,128]{3,2,1,0:T(8,128)S(1)} %convert_multiply_fusion.1.refs_1_, ...), custom_call_target="tpu_custom_call" | custom-call | tf_op jit(solution)/shard_map/add/pallas_call | solution.py:236
  (11 shorter events, 0.2 us)
Async XLA Ops:
  0.6 5.9 %copy-start = (bf16[3,3,3,128,128]{4,3,2,1,0:T(8,128)(2,1)S(1)}, bf16[3,3,3,128,128]{4,3,2,1,0:T(8,128)(2,1)}, u32[]{:S(2)}) copy-start(bf16[3,3,3,128,128]{4,3,2,1,0:T(8,128)(2,1)} %param.10) | copy-start | bytes 2654212
  1.8 7.9 %collective-permute-start = (bf16[2,8,2,16,128]{4,3,2,1,0:T(8,128)(2,1)S(1)}, bf16[2,8,2,16,128]{4,3,2,1,0:T(8,128)(2,1)S(1)}, u32[]{:S(2)}, u32[]{:S(2)}) collective-permute-start(bf16[2,8,2,16,128]{4,3,2,1,0:T(8,128)(2,1)S(1)} %maximum_bitcast_fusion.1.refs_0_), channel_id=1, source_target_pairs={{0,24},{4,28},{8,16},{12,20},{16,8},{20,12},{24,0},{28,4},{1,25},{... | collective-permute-start | bytes 393224 | tf_op jit(solution)/shard_map/ppermute | solution.py:167
  5.8 7.1 %collective-permute-start.1 = (bf16[2,8,2,16,128]{4,3,2,1,0:T(8,128)(2,1)S(1)}, bf16[2,8,2,16,128]{4,3,2,1,0:T(8,128)(2,1)S(1)}, u32[]{:S(2)}, u32[]{:S(2)}) collective-permute-start(bf16[2,8,2,16,128]{4,3,2,1,0:T(8,128)(2,1)S(1)} %maximum_bitcast_fusion.1.refs_0_), channel_id=1, source_target_pairs={{0,4},{4,0},{8,12},{12,8},{16,20},{20,16},{24,28},{28,24},{1,5},{5... | collective-permute-start | bytes 393224 | tf_op jit(solution)/shard_map/ppermute | solution.py:167
  5.8 6.6 %collective-permute-start.3 = (bf16[2,8,2,16,128]{4,3,2,1,0:T(8,128)(2,1)S(1)}, bf16[2,8,2,16,128]{4,3,2,1,0:T(8,128)(2,1)S(1)}, u32[]{:S(2)}, u32[]{:S(2)}) collective-permute-start(bf16[2,8,2,16,128]{4,3,2,1,0:T(8,128)(2,1)S(1)} %maximum_bitcast_fusion.1.refs_0_), channel_id=1, source_target_pairs={{0,8},{4,12},{8,0},{12,4},{16,24},{20,28},{24,16},{28,20},{1,9},{5... | collective-permute-start | bytes 393224 | tf_op jit(solution)/shard_map/ppermute | solution.py:167
  6.3 6.0 %collective-permute-start.5 = (bf16[2,8,2,16,128]{4,3,2,1,0:T(8,128)(2,1)S(1)}, bf16[2,8,2,16,128]{4,3,2,1,0:T(8,128)(2,1)S(1)}, u32[]{:S(2)}, u32[]{:S(2)}) collective-permute-start(bf16[2,8,2,16,128]{4,3,2,1,0:T(8,128)(2,1)S(1)} %maximum_bitcast_fusion.1.refs_0_), channel_id=1, source_target_pairs={{0,16},{4,20},{8,24},{12,28},{16,0},{20,4},{24,8},{28,12},{1,17},{... | collective-permute-start | bytes 393224 | tf_op jit(solution)/shard_map/ppermute | solution.py:167
  7.2 0.7 %copy-start.1 = (s32[512]{0:T(512)S(1)}, s32[512]{0:T(512)}, u32[]{:S(2)}) copy-start(s32[512]{0:T(512)} %constant.33.clone) | copy-start | bytes 6148
  7.2 0.7 %copy-start.2 = (s32[512]{0:T(512)S(1)}, s32[512]{0:T(512)}, u32[]{:S(2)}) copy-start(s32[512]{0:T(512)} %constant.40) | copy-start | bytes 6148
  7.2 0.7 %copy-start.3 = (pred[512]{0:T(512)(128)(4,1)S(1)}, pred[512]{0:T(512)(128)(4,1)}, u32[]{:S(2)}) copy-start(pred[512]{0:T(512)(128)(4,1)} %constant.38) | copy-start | bytes 1540
  9.7 3.1 %collective-permute-start.2 = (bf16[2,8,2,16,128]{4,3,2,1,0:T(8,128)(2,1)S(1)}, bf16[2,8,2,16,128]{4,3,2,1,0:T(8,128)(2,1)S(1)}, u32[]{:S(2)}, u32[]{:S(2)}) collective-permute-start(bf16[2,8,2,16,128]{4,3,2,1,0:T(8,128)(2,1)S(1)} %collective-permute-done.refs_2_), channel_id=1, source_target_pairs={{0,4},{4,0},{8,12},{12,8},{16,20},{20,16},{24,28},{28,24},{1,5},{5... | collective-permute-start | bytes 393224 | tf_op jit(solution)/shard_map/ppermute | solution.py:167
  12.3 1.3 %collective-permute-start.4 = (bf16[2,8,2,16,128]{4,3,2,1,0:T(8,128)(2,1)S(1)}, bf16[2,8,2,16,128]{4,3,2,1,0:T(8,128)(2,1)S(1)}, u32[]{:S(2)}, u32[]{:S(2)}) collective-permute-start(bf16[2,8,2,16,128]{4,3,2,1,0:T(8,128)(2,1)S(1)} %collective-permute-done.3.refs_0_), channel_id=1, source_target_pairs={{0,4},{4,0},{8,12},{12,8},{16,20},{20,16},{24,28},{28,24},{1,5},{5... | collective-permute-start | bytes 393224 | tf_op jit(solution)/shard_map/ppermute | solution.py:167
  12.3 1.5 %collective-permute-start.6 = (bf16[2,8,2,16,128]{4,3,2,1,0:T(8,128)(2,1)S(1)}, bf16[2,8,2,16,128]{4,3,2,1,0:T(8,128)(2,1)S(1)}, u32[]{:S(2)}, u32[]{:S(2)}) collective-permute-start(bf16[2,8,2,16,128]{4,3,2,1,0:T(8,128)(2,1)S(1)} %collective-permute-done.5.refs_2_), channel_id=1, source_target_pairs={{0,4},{4,0},{8,12},{12,8},{16,20},{20,16},{24,28},{28,24},{1,5},{5... | collective-permute-start | bytes 393224 | tf_op jit(solution)/shard_map/ppermute | solution.py:167
  14.6 5.5 %collective-permute-start.9 = (f16[2,8,16,128]{3,2,1,0:T(8,128)(2,1)S(1)}, f16[2,8,16,128]{3,2,1,0:T(8,128)(2,1)S(1)}, u32[]{:S(2)}, u32[]{:S(2)}) collective-permute-start(f16[2,8,16,128]{3,2,1,0:T(8,128)(2,1)S(1)} %multiply_convert_fusion), channel_id=1, source_target_pairs={{0,4},{1,5},{2,3},{3,2},{4,0},{5,1},{6,7},{7,6},{8,12},{9,13},{10,... | collective-permute-start | bytes 196616 | tf_op jit(solution)/shard_map/ppermute | solution.py:229
  15.0 5.1 %collective-permute-start.8 = (f16[2,8,16,128]{3,2,1,0:T(8,128)(2,1)S(1)}, f16[2,8,16,128]{3,2,1,0:T(8,128)(2,1)S(1)}, u32[]{:S(2)}, u32[]{:S(2)}) collective-permute-start(f16[2,8,16,128]{3,2,1,0:T(8,128)(2,1)S(1)} %multiply_convert_fusion.1), channel_id=1, source_target_pairs={{0,4},{1,2},{2,1},{3,7},{4,0},{5,6},{6,5},{7,3},{8,12},{9,10},{10,... | collective-permute-start | bytes 196616 | tf_op jit(solution)/shard_map/ppermute | solution.py:229
  15.3 6.5 %collective-permute-start.7 = (f16[2,8,16,128]{3,2,1,0:T(8,128)(2,1)S(1)}, f16[2,8,16,128]{3,2,1,0:T(8,128)(2,1)S(1)}, u32[]{:S(2)}, u32[]{:S(2)}) collective-permute-start(f16[2,8,16,128]{3,2,1,0:T(8,128)(2,1)S(1)} %multiply_convert_fusion.2), channel_id=1, source_target_pairs={{0,1},{1,0},{2,6},{3,7},{4,5},{5,4},{6,2},{7,3},{8,9},{9,8},{10,14... | collective-permute-start | bytes 196616 | tf_op jit(solution)/shard_map/ppermute | solution.py:229

commit v5 on v4

--- a/solution.py
+++ b/solution.py
@@ -104,19 +104,21 @@
 
 def edge_kernel(count, start, lhs_ref, sum_ref, *refs):
     blocks, edge_refs = refs[:count], refs[count:]
-    arrays, rows, planes, width, _ = blocks[0].shape
+    arrays, rows, planes, width, cols = blocks[0].shape
     depth = 3 * count * width
     slab = lax.axis_index("slab")
 
-    def edge(a, r, t, p):
-        lhs = lhs_ref[a, t * 3 * width : (t + 1) * 3 * width, start : start + depth]
-        y = jnp.dot(lhs, window(blocks, a, r, [p]), preferred_element_type=F32)
-        return columns([y[k * width : (k + 1) * width] for k in range(3)])
-
     for a in range(arrays):
+        taps = [lhs_ref[a, t * 3 * width : (t + 1) * 3 * width, start : start + depth] for t in (2, 0)]
+        lhs = jnp.concatenate(taps, axis=0)
         for r in range(rows):
-            below = edge(a, r, 2, 0) + sum_ref[a, r, 0]
-            above = edge(a, r, 0, planes - 1) + sum_ref[a, r, planes + 1]
+            y = jnp.dot(lhs, window(blocks, a, r, (0, planes - 1)), preferred_element_type=F32)
+            below, above = (
+                columns([y[(3 * i + k) * width : (3 * i + k + 1) * width, i * cols : (i + 1) * cols] for k in range(3)])
+                for i in range(2)
+            )
+            below = below + sum_ref[a, r, 0]
+            above = above + sum_ref[a, r, planes + 1]
             for j, edge_ref in enumerate(edge_refs):
                 edge_ref[a, r] = jnp.where(lax.rem(slab, ROUNDS) == j, above, below)
 

time: 22.7 us -> 22.5 us (level)
  Pallas kernels: 2.52 us -> 2.27 us
    pallas_call x3, Pallas kernels: 1.78 us -> 1.53 us  [call(): pl.pallas_call(kernel, out_shape=out_shape, in_specs=[pl.BlockSpec(memory...]
where the time goes in v5:
time: 22.5 us; the launch traced here: 22.3 us
  starting transfers between devices  10.1 us (45%)
  waiting for transfers between devices  6.14 us (27%)
  Pallas kernels  2.27 us (10%)
  local copies, waits for them, and re-layouts  1.33 us (6%)
  other arithmetic  1.24 us (6%)
  between operations  0.8 us (4%)
  matrix products  0.37 us (2%)
    ppermute x7, starting transfers between devices, swap(): return lax.ppermute(value, 'chan', [(i, i ^ bit) for i in range(devices)])  5.22 us
    ppermute x3, starting transfers between devices, exchange(): value = lax.ppermute(value, ('chan', 'slab'), pairs)  4.93 us
    ppermute x7, waiting for transfers between devices, swap(): return lax.ppermute(value, 'chan', [(i, i ^ bit) for i in range(devices)])  4.5 us
    ppermute x3, waiting for transfers between devices, exchange(): value = lax.ppermute(value, ('chan', 'slab'), pairs)  1.64 us
    pallas_call x3, Pallas kernels, call(): pl.pallas_call(kernel, out_shape=out_shape, in_specs=[pl.BlockSpec(memory...  1.53 us
    another operation x1, other arithmetic, aligned_body(): own = jnp.stack([activations, masked]).transpose(0, 3, 2, 1, 4)  1.1 us
    unnamed x9, local copies, waits for them, and re-layouts  0.85 us
    pallas_call x1, Pallas kernels, aligned_body(): pl.pallas_call(add_kernel, out_shape=(out, out), in_specs=[pl.BlockSpec(m...  0.74 us
  transfers between devices with their start and end apart: 10, of which 5 were waited for; matrix products, arithmetic and copies ran while one was open for 6% of the time, Pallas kernels for 5%

profile of v5, /device:TPU:0, one launch (start us, length us, event | category | flops | bytes accessed | tf_op | source)
XLA Modules:
  0.0 22.3 jit_solution(1198586968318462442)
XLA Ops:
  0.6 0.0 copy-start
  0.6 1.1 %fusion.4 = (bf16[1,16,2,8,128]{4,1,2,3,0:T(8,128)(2,1)S(1)}, bf16[1,16,2,8,128]{4,1,2,3,0:T(8,128)(2,1)S(1)}) fusion(s32[16,2,8,128]{3,2,1,0:T(8,128)} %param.9, bf16[16,2,8,128]{3,2,1,0:T(8,128)(2,1)} %param.8, bf16[16,2,8,128]{3,2,1,0:T(8,128)(2,1)} %param.7), kind=kLoop, calls=%fused_computation.17 | loop fusion | flops 65536 | bytes 393216 | tf_op jit(solution)/shard_map/stack | solution.py:166
  1.8 4.0 %collective-permute-start = (bf16[2,8,2,16,128]{4,3,2,1,0:T(8,128)(2,1)S(1)}, bf16[2,8,2,16,128]{4,3,2,1,0:T(8,128)(2,1)S(1)}, u32[]{:S(2)}, u32[]{:S(2)}) collective-permute-start(bf16[2,8,2,16,128]{4,3,2,1,0:T(8,128)(2,1)S(1)} %maximum_bitcast_fusion.1.refs_0_), channel_id=1, source_target_pairs={{0,24},{4,28},{8,16},{12,20},{16,8},{20,12},{24,0},{28,4},{1,25},{... | collective-permute-start | bytes 393224 | tf_op jit(solution)/shard_map/ppermute | solution.py:169
  5.8 0.0 collective-permute-start.1
  5.8 0.5 %collective-permute-start.3 = (bf16[2,8,2,16,128]{4,3,2,1,0:T(8,128)(2,1)S(1)}, bf16[2,8,2,16,128]{4,3,2,1,0:T(8,128)(2,1)S(1)}, u32[]{:S(2)}, u32[]{:S(2)}) collective-permute-start(bf16[2,8,2,16,128]{4,3,2,1,0:T(8,128)(2,1)S(1)} %maximum_bitcast_fusion.1.refs_0_), channel_id=1, source_target_pairs={{0,8},{4,12},{8,0},{12,4},{16,24},{20,28},{24,16},{28,20},{1,9},{5... | collective-permute-start | bytes 393224 | tf_op jit(solution)/shard_map/ppermute | solution.py:169
  6.3 0.2 collective-permute-start.5
  6.5 0.0 copy-done
  6.5 0.3 %constant_dynamic-slice_fusion = bf16[3,3,3,128,16]{4,3,2,1,0:T(8,128)(2,1)S(1)} fusion(bf16[3,3,3,128,128]{4,3,2,1,0:T(8,128)(2,1)S(1)} %copy-done, s32[]{:T(128)S(6)} %select_n.13), kind=kLoop, calls=%fused_computation.20 | loop fusion | bytes 221188 | tf_op jit(solution)/shard_map/dynamic_slice | solution.py:178
  6.8 0.3 %copy.23 = bf16[3,3,3,128,16]{3,4,2,1,0:T(8,128)(2,1)S(1)} copy(bf16[3,3,3,128,16]{4,3,2,1,0:T(8,128)(2,1)S(1)} %constant_dynamic-slice_fusion) | data formatting | bytes 221184
  7.2 0.0 copy-start.1
  7.2 0.0 copy-start.2
  7.2 0.0 copy-start.3
  7.2 0.1 copy.22
  7.4 0.5 %copy-done.1 = s32[512]{0:T(512)S(1)} copy-done((s32[512]{0:T(512)S(1)}, s32[512]{0:T(512)}, u32[]{:S(2)}) %copy-start.1) | copy-done | bytes 2072
  7.9 0.0 copy-done.2
  7.9 0.0 copy-done.3
  7.9 0.4 %convolution_convert_fusion = bf16[288,512]{1,0:T(8,128)(2,1)S(1)} fusion(s32[512]{0:T(512)S(1)} %add_select_fusion, bf16[36,8,3,128]{3,2,1,0:T(4,128)(2,1)S(1)} %bitcast.23), kind=kOutput, calls=%fused_computation | convolution fusion | flops 113590272 | bytes 518144 | tf_op jit(solution)/shard_map/dot_general | solution.py:192
  8.3 1.4 %collective-permute-done.refs_2_ = bf16[2,8,2,16,128]{4,3,2,1,0:T(8,128)(2,1)S(1)} collective-permute-done((bf16[2,8,2,16,128]{4,3,2,1,0:T(8,128)(2,1)S(1)}, bf16[2,8,2,16,128]{4,3,2,1,0:T(8,128)(2,1)S(1)}, u32[]{:S(2)}, u32[]{:S(2)}) %collective-permute-start) | collective-permute-done | bytes 131104 | tf_op jit(solution)/shard_map/ppermute | solution.py:169
  9.7 0.0 collective-permute-start.2
  9.7 2.6 %collective-permute-done.3.refs_0_ = bf16[2,8,2,16,128]{4,3,2,1,0:T(8,128)(2,1)S(1)} collective-permute-done((bf16[2,8,2,16,128]{4,3,2,1,0:T(8,128)(2,1)S(1)}, bf16[2,8,2,16,128]{4,3,2,1,0:T(8,128)(2,1)S(1)}, u32[]{:S(2)}, u32[]{:S(2)}) %collective-permute-start.3) | collective-permute-done | bytes 131104 | tf_op jit(solution)/shard_map/ppermute | solution.py:169
  12.3 0.0 collective-permute-start.4
  12.3 0.0 collective-permute-done.5.refs_2_
  12.3 0.5 %collective-permute-start.6 = (bf16[2,8,2,16,128]{4,3,2,1,0:T(8,128)(2,1)S(1)}, bf16[2,8,2,16,128]{4,3,2,1,0:T(8,128)(2,1)S(1)}, u32[]{:S(2)}, u32[]{:S(2)}) collective-permute-start(bf16[2,8,2,16,128]{4,3,2,1,0:T(8,128)(2,1)S(1)} %collective-permute-done.5.refs_2_), channel_id=1, source_target_pairs={{0,4},{4,0},{8,12},{12,8},{16,20},{20,16},{24,28},{28,24},{1,5},{5... | collective-permute-start | bytes 393224 | tf_op jit(solution)/shard_map/ppermute | solution.py:169
  12.8 0.0 collective-permute-done.1.refs_1_
  12.8 0.0 collective-permute-done.2.refs_3_
  12.8 0.5 %shard_map.86.sum_ref = f32[2,8,4,16,128]{4,3,2,1,0:T(8,128)S(1)} custom-call(bf16[2,144,512]{2,1,0:T(8,128)(2,1)S(1)} %bitcast.20, bf16[2,8,2,16,128]{4,3,2,1,0:T(8,128)(2,1)S(1)} %maximum_bitcast_fusion.1.refs_0_, bf16[2,8,2,16,128]{4,3,2,1,0:T(8,128)(2,1)S(1)} %collective-permute-done.1.refs_1_, ...), custom_call_target="tpu_custom_call" | custom-call | flops 268435456 | bytes 1048576 | tf_op jit(solution)/shard_map/pallas_call | solution.py:203
  13.4 0.3 %collective-permute-done.4.refs_1_ = bf16[2,8,2,16,128]{4,3,2,1,0:T(8,128)(2,1)S(1)} collective-permute-done((bf16[2,8,2,16,128]{4,3,2,1,0:T(8,128)(2,1)S(1)}, bf16[2,8,2,16,128]{4,3,2,1,0:T(8,128)(2,1)S(1)}, u32[]{:S(2)}, u32[]{:S(2)}) %collective-permute-start.4) | collective-permute-done | bytes 131104 | tf_op jit(solution)/shard_map/ppermute | solution.py:169
  13.7 0.2 collective-permute-done.6.refs_3_
  13.8 0.4 %shard_map.88 = (f32[2,8,16,128]{3,2,1,0:T(8,128)S(1)}, f32[2,8,16,128]{3,2,1,0:T(8,128)S(1)}, f32[2,8,16,128]{3,2,1,0:T(8,128)S(1)}) custom-call(bf16[2,144,512]{2,1,0:T(8,128)(2,1)S(1)} %bitcast.21, f32[2,8,4,16,128]{4,3,2,1,0:T(8,128)S(1)} %shard_map.86.sum_ref, bf16[2,8,2,16,128]{4,3,2,1,0:T(8,128)(2,1)S(1)} %collective-permute-done.3.refs_0_, ...), custom_call_target="tpu_custom_call" | custom-call | flops 268435456 | bytes 1048576 | tf_op jit(solution)/shard_map/pallas_call | solution.py:203
  14.3 0.4 %collective-permute-start.9 = (f16[2,8,16,128]{3,2,1,0:T(8,128)(2,1)S(1)}, f16[2,8,16,128]{3,2,1,0:T(8,128)(2,1)S(1)}, u32[]{:S(2)}, u32[]{:S(2)}) collective-permute-start(f16[2,8,16,128]{3,2,1,0:T(8,128)(2,1)S(1)} %multiply_convert_fusion), channel_id=1, source_target_pairs={{0,4},{1,5},{2,3},{3,2},{4,0},{5,1},{6,7},{7,6},{8,12},{9,13},{10,... | collective-permute-start | bytes 196616 | tf_op jit(solution)/shard_map/ppermute | solution.py:231
  14.7 0.2 %collective-permute-start.8 = (f16[2,8,16,128]{3,2,1,0:T(8,128)(2,1)S(1)}, f16[2,8,16,128]{3,2,1,0:T(8,128)(2,1)S(1)}, u32[]{:S(2)}, u32[]{:S(2)}) collective-permute-start(f16[2,8,16,128]{3,2,1,0:T(8,128)(2,1)S(1)} %multiply_convert_fusion.1), channel_id=1, source_target_pairs={{0,4},{1,2},{2,1},{3,7},{4,0},{5,6},{6,5},{7,3},{8,12},{9,10},{10,... | collective-permute-start | bytes 196616 | tf_op jit(solution)/shard_map/ppermute | solution.py:231
  15.0 4.3 %collective-permute-start.7 = (f16[2,8,16,128]{3,2,1,0:T(8,128)(2,1)S(1)}, f16[2,8,16,128]{3,2,1,0:T(8,128)(2,1)S(1)}, u32[]{:S(2)}, u32[]{:S(2)}) collective-permute-start(f16[2,8,16,128]{3,2,1,0:T(8,128)(2,1)S(1)} %multiply_convert_fusion.2), channel_id=1, source_target_pairs={{0,1},{1,0},{2,6},{3,7},{4,5},{5,4},{6,2},{7,3},{8,9},{9,8},{10,14... | collective-permute-start | bytes 196616 | tf_op jit(solution)/shard_map/ppermute | solution.py:231
  19.3 0.5 %shard_map.87.inner_ref = f32[2,8,2,16,128]{4,3,2,1,0:T(8,128)S(1)} custom-call(bf16[2,144,512]{2,1,0:T(8,128)(2,1)S(1)} %bitcast.22, f32[2,8,4,16,128]{4,3,2,1,0:T(8,128)S(1)} %shard_map.86.sum_ref, bf16[2,8,2,16,128]{4,3,2,1,0:T(8,128)(2,1)S(1)} %collective-permute-done.3.refs_0_, bf16[2,8,2,16,128]{4,3,2,1,0:T(8,128)(2,1)S(1)} %collective-permute-done.4.refs_1_, ...), custom_call_target="tpu_custom_call" | custom-call | flops 268435456 | bytes 1048576 | tf_op jit(solution)/shard_map/pallas_call | solution.py:203
  19.8 0.0 collective-permute-done.9
  19.9 0.0 collective-permute-done.8
  19.9 1.6 %collective-permute-done.7 = f16[2,8,16,128]{3,2,1,0:T(8,128)(2,1)S(1)} collective-permute-done((f16[2,8,16,128]{3,2,1,0:T(8,128)(2,1)S(1)}, f16[2,8,16,128]{3,2,1,0:T(8,128)(2,1)S(1)}, u32[]{:S(2)}, u32[]{:S(2)}) %collective-permute-start.7) | collective-permute-done | bytes 65568 | tf_op jit(solution)/shard_map/ppermute | solution.py:231
  21.6 0.7 %add.18 = (bf16[16,2,8,128]{3,2,1,0:T(8,128)(2,1)}, bf16[16,2,8,128]{3,2,1,0:T(8,128)(2,1)}) custom-call(f32[2,8,2,16,128]{4,3,2,1,0:T(8,128)S(1)} %shard_map.87.inner_ref, f32[2,8,16,128]{3,2,1,0:T(8,128)S(1)} %convert_multiply_fusion.2.refs_0_, f32[2,8,16,128]{3,2,1,0:T(8,128)S(1)} %convert_multiply_fusion.1.refs_1_, ...), custom_call_target="tpu_custom_call" | custom-call | tf_op jit(solution)/shard_map/add/pallas_call | solution.py:238
  (11 shorter events, 0.2 us)
Async XLA Ops:
  0.6 5.9 %copy-start = (bf16[3,3,3,128,128]{4,3,2,1,0:T(8,128)(2,1)S(1)}, bf16[3,3,3,128,128]{4,3,2,1,0:T(8,128)(2,1)}, u32[]{:S(2)}) copy-start(bf16[3,3,3,128,128]{4,3,2,1,0:T(8,128)(2,1)} %param.10) | copy-start | bytes 2654212
  1.8 7.9 %collective-permute-start = (bf16[2,8,2,16,128]{4,3,2,1,0:T(8,128)(2,1)S(1)}, bf16[2,8,2,16,128]{4,3,2,1,0:T(8,128)(2,1)S(1)}, u32[]{:S(2)}, u32[]{:S(2)}) collective-permute-start(bf16[2,8,2,16,128]{4,3,2,1,0:T(8,128)(2,1)S(1)} %maximum_bitcast_fusion.1.refs_0_), channel_id=1, source_target_pairs={{0,24},{4,28},{8,16},{12,20},{16,8},{20,12},{24,0},{28,4},{1,25},{... | collective-permute-start | bytes 393224 | tf_op jit(solution)/shard_map/ppermute | solution.py:169
  5.8 7.1 %collective-permute-start.1 = (bf16[2,8,2,16,128]{4,3,2,1,0:T(8,128)(2,1)S(1)}, bf16[2,8,2,16,128]{4,3,2,1,0:T(8,128)(2,1)S(1)}, u32[]{:S(2)}, u32[]{:S(2)}) collective-permute-start(bf16[2,8,2,16,128]{4,3,2,1,0:T(8,128)(2,1)S(1)} %maximum_bitcast_fusion.1.refs_0_), channel_id=1, source_target_pairs={{0,4},{4,0},{8,12},{12,8},{16,20},{20,16},{24,28},{28,24},{1,5},{5... | collective-permute-start | bytes 393224 | tf_op jit(solution)/shard_map/ppermute | solution.py:169
  5.8 6.6 %collective-permute-start.3 = (bf16[2,8,2,16,128]{4,3,2,1,0:T(8,128)(2,1)S(1)}, bf16[2,8,2,16,128]{4,3,2,1,0:T(8,128)(2,1)S(1)}, u32[]{:S(2)}, u32[]{:S(2)}) collective-permute-start(bf16[2,8,2,16,128]{4,3,2,1,0:T(8,128)(2,1)S(1)} %maximum_bitcast_fusion.1.refs_0_), channel_id=1, source_target_pairs={{0,8},{4,12},{8,0},{12,4},{16,24},{20,28},{24,16},{28,20},{1,9},{5... | collective-permute-start | bytes 393224 | tf_op jit(solution)/shard_map/ppermute | solution.py:169
  6.3 6.0 %collective-permute-start.5 = (bf16[2,8,2,16,128]{4,3,2,1,0:T(8,128)(2,1)S(1)}, bf16[2,8,2,16,128]{4,3,2,1,0:T(8,128)(2,1)S(1)}, u32[]{:S(2)}, u32[]{:S(2)}) collective-permute-start(bf16[2,8,2,16,128]{4,3,2,1,0:T(8,128)(2,1)S(1)} %maximum_bitcast_fusion.1.refs_0_), channel_id=1, source_target_pairs={{0,16},{4,20},{8,24},{12,28},{16,0},{20,4},{24,8},{28,12},{1,17},{... | collective-permute-start | bytes 393224 | tf_op jit(solution)/shard_map/ppermute | solution.py:169
  7.2 0.7 %copy-start.1 = (s32[512]{0:T(512)S(1)}, s32[512]{0:T(512)}, u32[]{:S(2)}) copy-start(s32[512]{0:T(512)} %constant.33.clone) | copy-start | bytes 6148
  7.2 0.7 %copy-start.2 = (s32[512]{0:T(512)S(1)}, s32[512]{0:T(512)}, u32[]{:S(2)}) copy-start(s32[512]{0:T(512)} %constant.40) | copy-start | bytes 6148
  7.2 0.7 %copy-start.3 = (pred[512]{0:T(512)(128)(4,1)S(1)}, pred[512]{0:T(512)(128)(4,1)}, u32[]{:S(2)}) copy-start(pred[512]{0:T(512)(128)(4,1)} %constant.38) | copy-start | bytes 1540
  9.7 3.1 %collective-permute-start.2 = (bf16[2,8,2,16,128]{4,3,2,1,0:T(8,128)(2,1)S(1)}, bf16[2,8,2,16,128]{4,3,2,1,0:T(8,128)(2,1)S(1)}, u32[]{:S(2)}, u32[]{:S(2)}) collective-permute-start(bf16[2,8,2,16,128]{4,3,2,1,0:T(8,128)(2,1)S(1)} %collective-permute-done.refs_2_), channel_id=1, source_target_pairs={{0,4},{4,0},{8,12},{12,8},{16,20},{20,16},{24,28},{28,24},{1,5},{5... | collective-permute-start | bytes 393224 | tf_op jit(solution)/shard_map/ppermute | solution.py:169
  12.3 1.3 %collective-permute-start.4 = (bf16[2,8,2,16,128]{4,3,2,1,0:T(8,128)(2,1)S(1)}, bf16[2,8,2,16,128]{4,3,2,1,0:T(8,128)(2,1)S(1)}, u32[]{:S(2)}, u32[]{:S(2)}) collective-permute-start(bf16[2,8,2,16,128]{4,3,2,1,0:T(8,128)(2,1)S(1)} %collective-permute-done.3.refs_0_), channel_id=1, source_target_pairs={{0,4},{4,0},{8,12},{12,8},{16,20},{20,16},{24,28},{28,24},{1,5},{5... | collective-permute-start | bytes 393224 | tf_op jit(solution)/shard_map/ppermute | solution.py:169
  12.3 1.5 %collective-permute-start.6 = (bf16[2,8,2,16,128]{4,3,2,1,0:T(8,128)(2,1)S(1)}, bf16[2,8,2,16,128]{4,3,2,1,0:T(8,128)(2,1)S(1)}, u32[]{:S(2)}, u32[]{:S(2)}) collective-permute-start(bf16[2,8,2,16,128]{4,3,2,1,0:T(8,128)(2,1)S(1)} %collective-permute-done.5.refs_2_), channel_id=1, source_target_pairs={{0,4},{4,0},{8,12},{12,8},{16,20},{20,16},{24,28},{28,24},{1,5},{5... | collective-permute-start | bytes 393224 | tf_op jit(solution)/shard_map/ppermute | solution.py:169
  14.3 5.5 %collective-permute-start.9 = (f16[2,8,16,128]{3,2,1,0:T(8,128)(2,1)S(1)}, f16[2,8,16,128]{3,2,1,0:T(8,128)(2,1)S(1)}, u32[]{:S(2)}, u32[]{:S(2)}) collective-permute-start(f16[2,8,16,128]{3,2,1,0:T(8,128)(2,1)S(1)} %multiply_convert_fusion), channel_id=1, source_target_pairs={{0,4},{1,5},{2,3},{3,2},{4,0},{5,1},{6,7},{7,6},{8,12},{9,13},{10,... | collective-permute-start | bytes 196616 | tf_op jit(solution)/shard_map/ppermute | solution.py:231
  14.7 5.1 %collective-permute-start.8 = (f16[2,8,16,128]{3,2,1,0:T(8,128)(2,1)S(1)}, f16[2,8,16,128]{3,2,1,0:T(8,128)(2,1)S(1)}, u32[]{:S(2)}, u32[]{:S(2)}) collective-permute-start(f16[2,8,16,128]{3,2,1,0:T(8,128)(2,1)S(1)} %multiply_convert_fusion.1), channel_id=1, source_target_pairs={{0,4},{1,2},{2,1},{3,7},{4,0},{5,6},{6,5},{7,3},{8,12},{9,10},{10,... | collective-permute-start | bytes 196616 | tf_op jit(solution)/shard_map/ppermute | solution.py:231
  15.0 6.5 %collective-permute-start.7 = (f16[2,8,16,128]{3,2,1,0:T(8,128)(2,1)S(1)}, f16[2,8,16,128]{3,2,1,0:T(8,128)(2,1)S(1)}, u32[]{:S(2)}, u32[]{:S(2)}) collective-permute-start(f16[2,8,16,128]{3,2,1,0:T(8,128)(2,1)S(1)} %multiply_convert_fusion.2), channel_id=1, source_target_pairs={{0,1},{1,0},{2,6},{3,7},{4,5},{5,4},{6,2},{7,3},{8,9},{9,8},{10,14... | collective-permute-start | bytes 196616 | tf_op jit(solution)/shard_map/ppermute | solution.py:231
